TPU v7x, 32 devices: a whole 2x2x4 slice. The times are simulated.
32 devices in a mesh: tenant: 8 (over z, x), tp: 4 (over y, core).
Axes of the slice: x: 2, y: 2, z: 4, core: 2. Of those that a mesh axis runs over, the one named last changes fastest.
Arguments:
- src_tokens: bfloat16 [96, 64, 1024], P('tenant'), may hold values from -64 to 64
- pair_tenant: int32 [96], P('tenant'), may hold values from 0 to 7, as said below
- pair_length: int32 [96], P('tenant'), may hold values from 1 to 64
- norm_gain: float32 [8, 1024], P('tenant'), may hold values from 0.1 to 1.9
- w_query: bfloat16 [8, 1024, 4096], P('tenant', None, 'tp'), may hold values from -1 to 1
- w_key: bfloat16 [8, 1024, 4096], P('tenant', None, 'tp'), may hold values from -1 to 1
- w_value: bfloat16 [8, 1024, 4096], P('tenant', None, 'tp'), may hold values from -0.1875 to 0.1875
- w_out: bfloat16 [8, 4096, 1024], P('tenant', 'tp'), may hold values from -0.09375 to 0.09375
- rel_bias: float32 [8, 32, 32], P('tenant', None, 'tp'), may hold values from -6 to 6
Outputs:
- layer_out: bfloat16 [4096, 1024], P(('tenant', 'tp'))
Inputs may be any that keep to these rules, and one draw needn't show every extreme that they name: `pair_tenant`: the pairs of one retriever shard bound for one tenant have pair_length summing to at most 64; in every draw some tenant receives exactly 64 tokens from every shard.
All inputs are finite; a program needn't handle non-finite values.
Results may differ from a plain program's by a relative error of at most 0.0065.
Values may be sent and summed in bfloat16 or wider, within the bound.
No kernel may reach another device: no remote copies, remote signals or barrier semaphores. Data moves between devices by JAX's collectives and lax.ppermute only.
A program may use at most 128 MiB of HBM per device.

v0:
```python
import functools
import math

import jax
import jax.numpy as jnp
import numpy as np
from jax import lax
from jax.experimental import pallas as pl
from jax.experimental.pallas import tpu as pltpu
from jax.sharding import PartitionSpec as P


LANES = 128
SEG_ROWS = 8
BLOCK = 256
MASKED = -1000000000.0
VMEM = pl.BlockSpec(memory_space=pltpu.VMEM)
SMEM = pl.BlockSpec(memory_space=pltpu.SMEM)
HBM = pl.BlockSpec(memory_space=pltpu.HBM)
MIB = 2**20


def in_vmem(value):
    return pltpu.with_memory_space_constraint(value, pltpu.VMEM)


def in_hbm(value):
    return pltpu.with_memory_space_constraint(value, pltpu.HBM)


def bucket_of(distance, buckets):
    half_count = buckets // 2
    exact_limit = half_count // 2
    size = abs(distance)
    if size < exact_limit:
        found = size
    else:
        found = exact_limit + int(
            np.floor(
                np.log(size / exact_limit)
                / math.log(128.0 / exact_limit)
                * (half_count - exact_limit)
            )
        )
        found = min(found, half_count - 1)
    return found + (half_count if distance > 0 else 0)


def bias_runs(extent, buckets):
    runs = []
    for distance in range(-extent + 1, extent):
        bucket = bucket_of(distance, buckets)
        if not runs or runs[-1][1] != bucket:
            runs.append((distance, bucket))
    return runs


def plan(tenants):
    half = tenants // 2
    split = half // 2
    far = [(tenants - 1 - i, tenants - 1 - i - split) for i in range(split)]
    near = [(half - 1 - i, half - 1 - i - split) for i in range(split - 1)]
    near.append((split, split))
    return far, near


def pick(core, pair):
    return pair[0] if pair[0] == pair[1] else jnp.where(core == 0, pair[0], pair[1])


def pack_kernel(rounds, cap, tenant_hbm, length_hbm, tokens_hbm, *refs):
    out_refs = refs[:-5]
    select, tokens_ref, tenant_ref, length_ref, semaphore = refs[-5:]
    pairs = tenant_ref.shape[0]
    columns = tokens_ref.shape[1]
    tables = [
        pltpu.make_async_copy(tenant_hbm, tenant_ref, semaphore.at[0]),
        pltpu.make_async_copy(length_hbm, length_ref, semaphore.at[1]),
    ]
    for copy in tables:
        copy.start()
    step = 2 * LANES
    fetches = []
    for i, at in enumerate(range(0, columns, step)):
        where = slice(at, at + step)
        fetches.append(
            pltpu.make_async_copy(
                tokens_hbm.at[:, where], tokens_ref.at[:, where], semaphore.at[2 + i]
            )
        )
        fetches[-1].start()
    for copy in tables:
        copy.wait()
    me = lax.axis_index("tenant")
    core = lax.rem(lax.axis_index("tp"), 2)
    side = LANES // cap
    lane = lax.broadcasted_iota(jnp.int32, (1, LANES), 1)
    place = lax.rem(lane, cap)
    part = lane // cap
    rows = lax.broadcasted_iota(jnp.int32, (cap, LANES), 0)
    for slot, pair in enumerate(rounds):
        bound = lax.bitwise_xor(me, jnp.int32(pick(core, pair)))
        offset = jnp.int32(0)
        seg = jnp.full((1, LANES), -1, jnp.int32)
        for group in range(pairs // side):
            first = jnp.zeros((1, LANES), jnp.int32)
            last = jnp.zeros((1, LANES), jnp.int32)
            for k in range(side):
                j = group * side + k
                live = jnp.where(tenant_ref[j] == bound, length_ref[j], 0)
                seg = jnp.where((place >= offset) & (place < offset + live), j, seg)
                first = jnp.where(part == k, offset, first)
                last = jnp.where(part == k, live, last)
                offset = offset + live
            target = jnp.where(place < last, first + place, -1)
            select[slot * cap : (slot + 1) * cap, group * LANES : (group + 1) * LANES] = (
                jnp.where(rows == target, 1.0, 0.0).astype(jnp.bfloat16)
            )
        out_refs[slot][columns // LANES * cap :, :] = jnp.broadcast_to(
            seg.astype(jnp.float32), (SEG_ROWS, LANES)
        ).astype(jnp.bfloat16)
    for fetch, at in zip(fetches, range(0, columns, step)):
        fetch.wait()
        packed = jnp.dot(
            select[...], tokens_ref[:, at : at + step], preferred_element_type=jnp.float32
        ).astype(jnp.bfloat16)
        for slot in range(len(rounds)):
            for c in range(step // LANES):
                block = at // LANES + c
                out_refs[slot][block * cap : (block + 1) * cap, :] = packed[
                    slot * cap : (slot + 1) * cap, c * LANES : (c + 1) * LANES
                ]


def prepare_kernel(runs, table_ref, *refs):
    count = (len(refs) - 2) // 2
    sources, bias_ref, targets, semaphore = refs[:count], refs[count], refs[count + 1 : -1], refs[-1]
    copies = []
    for i, (source, target) in enumerate(zip(sources, targets)):
        copies.append(pltpu.make_async_copy(source, target, semaphore.at[i]))
        copies[-1].start()
    heads, extent = bias_ref.shape[0], bias_ref.shape[1]
    distance = lax.broadcasted_iota(jnp.int32, (extent, extent), 1) - lax.broadcasted_iota(
        jnp.int32, (extent, extent), 0
    )
    for head in range(heads):
        value = jnp.full((extent, extent), table_ref[head, runs[0][1]], jnp.float32)
        for start, bucket in runs[1:]:
            value = jnp.where(distance >= start, table_ref[head, bucket], value)
        bias_ref[head] = value
    for copy in copies:
        copy.wait()


def sublayer_kernel(slots, far, cap, slot_count, *refs):
    slot_refs = refs[:slot_count]
    gain_ref, wq_ref, wk_ref, wv_ref, wo_ref, bias_ref = refs[slot_count : slot_count + 6]
    send_ref, keep_ref, x, seg, normed, q, k, v, context, score, top, weight = refs[
        slot_count + 6 :
    ]
    half, split = slot_count, slot_count // 2
    width = x.shape[1]
    me = lax.axis_index("tenant")
    t = lax.axis_index("tp")
    core, outer = lax.rem(t, 2), t // 2
    for ref, pair in zip(slot_refs, slots):
        slot = lax.bitwise_and(lax.bitwise_xor(me, jnp.int32(pick(core, pair))), half - 1)
        at = lax.bitwise_xor(slot, (1 - core) * split)
        for c in range(width // LANES):
            x[pl.ds(pl.multiple_of(at * cap, cap), cap), c * LANES : (c + 1) * LANES] = ref[
                c * cap : (c + 1) * cap, :
            ]
        seg[at] = ref[width // LANES * cap :, :].astype(jnp.float32)
    total = half * cap
    step = min(BLOCK, total)
    inner = min(LANES, total)
    side = inner // cap
    heads = bias_ref.shape[0]
    size = q.shape[1] // heads
    lane = lax.broadcasted_iota(jnp.int32, (1, inner), 1)
    diagonal = lax.broadcasted_iota(jnp.int32, (inner, inner), 0) == lax.broadcasted_iota(
        jnp.int32, (inner, inner), 1
    )
    owner = (me // half == outer) if not far else (me // half != outer)
    ones = jnp.ones((inner, size), jnp.bfloat16)
    scale = jnp.where(owner, 1.0, 0.0).astype(jnp.float32)
    for base in range(0, total, step):
        rows = slice(base, base + step)
        values = x[rows].astype(jnp.float32)
        mean_square = jnp.mean(values * values, axis=-1, keepdims=True)
        normed[...] = (values * lax.rsqrt(mean_square + 1e-06) * gain_ref[...]).astype(
            jnp.bfloat16
        )
        for w_ref, out in ((wq_ref, q), (wk_ref, k), (wv_ref, v)):
            out[...] = jnp.dot(
                normed[...], w_ref[...], preferred_element_type=jnp.float32
            ).astype(jnp.bfloat16)
        blocks = step // inner
        for block in range(blocks):
            first = (base + block * inner) // cap
            code = jnp.full((1, inner), -1.0, jnp.float32)
            for s in range(side):
                one = seg[first + s][:1, :inner]
                one = jnp.where(one >= 0.0, one + 1024.0 * s, -1.0)
                code = jnp.where(lane // cap == s, one, code)
            down = jnp.sum(jnp.where(diagonal, code, 0.0), axis=1, keepdims=True)
            allowed = down == jnp.where(code >= 0.0, code, -2.0)
            alive = jnp.broadcast_to(down >= 0.0, (inner, inner))
            at = slice(block * inner, (block + 1) * inner)
            for head in range(heads):
                cols = slice(head * size, (head + 1) * size)
                scores = lax.dot_general(
                    q[at, cols],
                    k[at, cols],
                    (((1,), (1,)), ((), ())),
                    preferred_element_type=jnp.float32,
                )
                scores = jnp.where(allowed, scores + bias_ref[head], MASKED)
                score[head] = scores
                top[head] = jnp.broadcast_to(
                    jnp.max(scores, axis=-1, keepdims=True), (inner, inner)
                )
            for head in range(heads):
                weight[head] = jnp.exp(score[head] - top[head]).astype(jnp.bfloat16)
            for head in range(heads):
                cols = slice(head * size, (head + 1) * size)
                both = jnp.dot(
                    weight[head],
                    jnp.concatenate([v[at, cols], ones], axis=1),
                    preferred_element_type=jnp.float32,
                )
                context[at, cols] = jnp.where(
                    alive, both[:, :size] * (1.0 / both[:, size:]), 0.0
                ).astype(jnp.bfloat16)
        partial = jnp.dot(context[...], wo_ref[...], preferred_element_type=jnp.float32)
        for at in range(0, step, split * cap) if step > split * cap else (0,):
            size_out = min(step, split * cap)
            row = base + at
            piece = partial[at : at + size_out]
            if row < split * cap:
                send_ref[row : row + size_out] = piece.astype(jnp.bfloat16)
            else:
                keep_ref[row - split * cap : row - split * cap + size_out] = (
                    piece + scale * x[row : row + size_out].astype(jnp.float32)
                )


def per_device(
    tenants,
    tp,
    src_tokens,
    pair_tenant,
    pair_length,
    norm_gain,
    w_query,
    w_key,
    w_value,
    w_out,
    rel_bias,
):
    pairs, cap, width = src_tokens.shape
    half, split = tenants // 2, tenants // 4
    far, near = plan(tenants)
    rounds = far + near + [(0, 0)]
    slot_shape = pltpu.VMEM((width // LANES * cap + SEG_ROWS, LANES), jnp.bfloat16)
    packed = pl.pallas_call(
        functools.partial(pack_kernel, rounds, cap),
        out_shape=[slot_shape] * len(rounds),
        in_specs=[HBM, HBM, HBM],
        out_specs=[VMEM] * len(rounds),
        scratch_shapes=[
            pltpu.VMEM((len(rounds) * cap, pairs * cap), jnp.bfloat16),
            pltpu.VMEM((pairs * cap, width), jnp.bfloat16),
            pltpu.SMEM((pairs,), jnp.int32),
            pltpu.SMEM((pairs,), jnp.int32),
            pltpu.SemaphoreType.DMA((2 + width // (2 * LANES),)),
        ],
        compiler_params=pltpu.CompilerParams(
            vmem_limit_bytes=2 * MIB + 2 * pairs * cap * (width + (len(rounds) + 1) * cap)
        ),
        name="pack",
    )(*map(in_hbm, (pair_tenant, pair_length, src_tokens.reshape(pairs * cap, width))))

    def shift(value, pair):
        moves = []
        for u in range(tenants):
            for t in range(tp):
                moves.append((u * tp + t, (u ^ pair[t % 2]) * tp + t))
        return lax.ppermute(value, ("tenant", "tp"), moves)

    def swap(value):
        return lax.ppermute(value, "tp", [(t, t ^ 1) for t in range(tp)])

    arrived = []
    for value, pair in zip(packed, rounds[:-1]):
        arrived.append(shift(value, pair))

    heads = rel_bias.shape[2]
    extent = min(LANES, half * cap)
    raw = [w[0] for w in (w_query, w_key, w_value, w_out)]
    bias, *weights = pl.pallas_call(
        functools.partial(prepare_kernel, bias_runs(extent, rel_bias.shape[1])),
        out_shape=[pltpu.VMEM((heads, extent, extent), jnp.float32)]
        + [pltpu.VMEM(w.shape, w.dtype) for w in raw],
        in_specs=[SMEM] + [HBM] * len(raw),
        out_specs=[VMEM] * (1 + len(raw)),
        scratch_shapes=[pltpu.SemaphoreType.DMA((len(raw),))],
        compiler_params=pltpu.CompilerParams(vmem_limit_bytes=4 * MIB),
        name="prepare",
    )(rel_bias[0].T, *map(in_hbm, raw))

    def sublayer(rounds_here, values, is_far):
        slots, arrays = [], []
        for pair, value in zip(rounds_here, values):
            slots.append(pair)
            arrays.append(value)
            if pair[0] != pair[1]:
                slots.append(pair[::-1])
                arrays.append(swap(value))
        total = half * cap
        step = min(BLOCK, total)
        own = w_query.shape[2]
        vmem = 8 * MIB + 4 * total * width
        return pl.pallas_call(
            functools.partial(sublayer_kernel, slots, is_far, cap, half),
            out_shape=[
                pltpu.VMEM((split * cap, width), jnp.bfloat16),
                pltpu.VMEM((split * cap, width), jnp.float32),
            ],
            in_specs=[VMEM] * (half + 6),
            out_specs=[VMEM, VMEM],
            scratch_shapes=[
                pltpu.VMEM((total, width), jnp.bfloat16),
                pltpu.VMEM((half, SEG_ROWS, LANES), jnp.float32),
                pltpu.VMEM((step, width), jnp.bfloat16),
                pltpu.VMEM((step, own), jnp.bfloat16),
                pltpu.VMEM((step, own), jnp.bfloat16),
                pltpu.VMEM((step, own), jnp.bfloat16),
                pltpu.VMEM((step, own), jnp.bfloat16),
                pltpu.VMEM((heads, extent, extent), jnp.float32),
                pltpu.VMEM((heads, extent, extent), jnp.float32),
                pltpu.VMEM((heads, extent, extent), jnp.bfloat16),
            ],
            compiler_params=pltpu.CompilerParams(vmem_limit_bytes=vmem),
            name="far" if is_far else "near",
        )(*[in_vmem(value) for value in arrays], norm_gain, *map(in_vmem, weights), in_vmem(bias))

    def cross(value, is_far):
        moves = []
        for u in range(tenants):
            for t in range(tp):
                owner = (u // half == t // 2) != is_far
                if not owner:
                    moves.append((u * tp + t, u * tp + (t ^ 2)))
        return lax.ppermute(value, ("tenant", "tp"), moves)

    def reduced(rounds_here, values, is_far):
        send, keep = sublayer(rounds_here, values, is_far)
        other = swap(send)
        pair_sum = keep + other.astype(jnp.float32)
        return pair_sum, cross(pair_sum.astype(jnp.bfloat16), is_far)

    near_sum, near_other = reduced(near + [(0, 0)], arrived[len(far) :] + [packed[-1]], False)
    far_sum, far_other = reduced(far, arrived[: len(far)], True)
    owner = lax.axis_index("tenant") // half == lax.axis_index("tp") // 2
    return jnp.where(
        owner,
        near_sum + near_other.astype(jnp.float32),
        far_sum + far_other.astype(jnp.float32),
    ).astype(jnp.bfloat16)


def solution(mesh):
    in_specs = (
        P("tenant", None, None),
        P("tenant"),
        P("tenant"),
        P("tenant", None),
        P("tenant", None, "tp"),
        P("tenant", None, "tp"),
        P("tenant", None, "tp"),
        P("tenant", "tp", None),
        P("tenant", None, "tp"),
    )
    out_specs = P(("tenant", "tp"), None)
    tenants = mesh.shape["tenant"]

    def body(*args):
        return per_device(tenants, mesh.shape["tp"], *args)

    return jax.shard_map(
        body, mesh=mesh, in_specs=in_specs, out_specs=out_specs, check_vma=False
    )
```

profile of v0, /device:TPU:0, one launch (start us, length us, event | category | flops | bytes accessed | tf_op | source)
XLA Modules:
  0.0 53.4 jit_solution(5517656187238861136)
XLA Ops:
  0.0 2.7 %pack.1 = (bf16[520,128]{1,0:T(8,128)(2,1)S(1)}, bf16[520,128]{1,0:T(8,128)(2,1)S(1)}, bf16[520,128]{1,0:T(8,128)(2,1)S(1)}, bf16[520,128]{1,0:T(8,128)(2,1)S(1)}, bf16[520,128]{1,0:T(8,128)(2,1)S(1)}) custom-call(s32[12]{0:T(128)} %tenant_hbm.1, s32[12]{0:T(128)} %length_hbm.1, bf16[768,1024]{1,0:T(8,128)(2,1)} %bitcast.13), custom_call_target="tpu_custom_call" | custom-call | tf_op jit(solution)/shard_map/pack/pallas_call | solution.py:266
  2.7 6.1 %collective-permute-start.5 = (bf16[520,128]{1,0:T(8,128)(2,1)S(1)}, bf16[520,128]{1,0:T(8,128)(2,1)S(1)}, u32[]{:S(2)}, u32[]{:S(2)}) collective-permute-start(bf16[520,128]{1,0:T(8,128)(2,1)S(1)} %get-tuple-element.29), channel_id=1, source_target_pairs={{0,28},{1,21},{2,30},{3,23},{4,24},{5,17},{6,26},{7,19},{8,20},{9,... | collective-permute-start | bytes 399368 | tf_op jit(solution)/shard_map/ppermute | solution.py:289
  8.7 0.2 collective-permute-start.7
  9.0 4.0 %collective-permute-done.5.refs_0_ = bf16[520,128]{1,0:T(8,128)(2,1)S(1)} collective-permute-done((bf16[520,128]{1,0:T(8,128)(2,1)S(1)}, bf16[520,128]{1,0:T(8,128)(2,1)S(1)}, u32[]{:S(2)}, u32[]{:S(2)}) %collective-permute-start.5) | collective-permute-done | bytes 133152 | tf_op jit(solution)/shard_map/ppermute | solution.py:289
  13.0 2.7 %collective-permute-start.6 = (bf16[520,128]{1,0:T(8,128)(2,1)S(1)}, bf16[520,128]{1,0:T(8,128)(2,1)S(1)}, u32[]{:S(2)}, u32[]{:S(2)}) collective-permute-start(bf16[520,128]{1,0:T(8,128)(2,1)S(1)} %collective-permute-done.5.refs_0_), channel_id=1, source_target_pairs={{0,1},{1,0},{2,3},{3,2},{4,5},{5,4},{6,7},{7,6},{8,9},{9,8},{10,11... | collective-permute-start | bytes 399368 | tf_op jit(solution)/shard_map/ppermute | solution.py:292
  15.7 0.0 collective-permute-done.7.refs_2_
  15.7 2.9 %collective-permute-start.8 = (bf16[520,128]{1,0:T(8,128)(2,1)S(1)}, bf16[520,128]{1,0:T(8,128)(2,1)S(1)}, u32[]{:S(2)}, u32[]{:S(2)}) collective-permute-start(bf16[520,128]{1,0:T(8,128)(2,1)S(1)} %collective-permute-done.7.refs_2_), channel_id=1, source_target_pairs={{0,1},{1,0},{2,3},{3,2},{4,5},{5,4},{6,7},{7,6},{8,9},{9,8},{10,11... | collective-permute-start | bytes 399368 | tf_op jit(solution)/shard_map/ppermute | solution.py:292
  18.6 2.0 %collective-permute-start = (bf16[520,128]{1,0:T(8,128)(2,1)S(1)}, bf16[520,128]{1,0:T(8,128)(2,1)S(1)}, u32[]{:S(2)}, u32[]{:S(2)}) collective-permute-start(bf16[520,128]{1,0:T(8,128)(2,1)S(1)} %get-tuple-element.19), channel_id=1, source_target_pairs={{0,12},{1,5},{2,14},{3,7},{4,8},{5,1},{6,10},{7,3},{8,4},{9,13},{1... | collective-permute-start | bytes 399368 | tf_op jit(solution)/shard_map/ppermute | solution.py:289
  20.6 0.0 copy-start.1
  20.6 0.7 %copy-done.1 = f32[1,32,8]{1,2,0:T(8,128)S(1)} copy-done((f32[1,32,8]{1,2,0:T(8,128)S(1)}, f32[1,32,8]{1,2,0:T(8,128)}, u32[]{:S(2)}) %copy-start.1) | copy-done | bytes 1048
  21.3 0.0 copy-start
  21.3 4.1 %prepare.1 = (f32[8,128,128]{2,1,0:T(8,128)S(1)}, bf16[1024,1024]{1,0:T(8,128)(2,1)S(1)}, bf16[1024,1024]{1,0:T(8,128)(2,1)S(1)}, bf16[1024,1024]{1,0:T(8,128)(2,1)S(1)}, bf16[1024,1024]{1,0:T(8,128)(2,1)S(1)}) custom-call(f32[8,32]{1,0:T(8,128)S(1)} %bitcast.8, bf16[1024,1024]{1,0:T(8,128)(2,1)} %bitcast.9, bf16[1024,1024]{1,0:T(8,128)(2,1)} %bitcast.10, ...), custom_call_target="tpu_custom_call" | custom-call | tf_op jit(solution)/shard_map/prepare/pallas_call | solution.py:301
  25.4 0.0 collective-permute-done.6.refs_1_
  25.4 0.0 collective-permute-done.8.refs_3_
  25.5 0.0 copy-done
  25.5 3.5 %far.1 = (bf16[128,1024]{1,0:T(8,128)(2,1)S(1)}, f32[128,1024]{1,0:T(8,128)S(1)}) custom-call(bf16[520,128]{1,0:T(8,128)(2,1)S(1)} %collective-permute-done.5.refs_0_, bf16[520,128]{1,0:T(8,128)(2,1)S(1)} %collective-permute-done.6.refs_1_, bf16[520,128]{1,0:T(8,128)(2,1)S(1)} %collective-permute-done.7.refs_2_, ...), custom_call_target="tpu_custom_call" | custom-call | tf_op jit(solution)/shard_map/far/pallas_call | solution.py:324
  29.0 0.1 collective-permute-start.9
  29.0 0.7 %collective-permute-start.2 = (bf16[520,128]{1,0:T(8,128)(2,1)S(1)}, bf16[520,128]{1,0:T(8,128)(2,1)S(1)}, u32[]{:S(2)}, u32[]{:S(2)}) collective-permute-start(bf16[520,128]{1,0:T(8,128)(2,1)S(1)} %get-tuple-element.20), channel_id=1, source_target_pairs={{0,8},{1,9},{2,10},{3,11},{4,12},{5,13},{6,14},{7,15},{8,0},{9,1},... | collective-permute-start | bytes 399368 | tf_op jit(solution)/shard_map/ppermute | solution.py:289
  29.7 0.0 collective-permute-done.refs_0_
  29.7 0.0 collective-permute-start.1
  29.8 5.2 %collective-permute-done.2.refs_2_ = bf16[520,128]{1,0:T(8,128)(2,1)S(1)} collective-permute-done((bf16[520,128]{1,0:T(8,128)(2,1)S(1)}, bf16[520,128]{1,0:T(8,128)(2,1)S(1)}, u32[]{:S(2)}, u32[]{:S(2)}) %collective-permute-start.2) | collective-permute-done | bytes 133152 | tf_op jit(solution)/shard_map/ppermute | solution.py:289
  35.0 0.0 collective-permute-done.1.refs_1_
  35.0 3.5 %near.1 = (bf16[128,1024]{1,0:T(8,128)(2,1)S(1)}, f32[128,1024]{1,0:T(8,128)S(1)}) custom-call(bf16[520,128]{1,0:T(8,128)(2,1)S(1)} %collective-permute-done.refs_0_, bf16[520,128]{1,0:T(8,128)(2,1)S(1)} %collective-permute-done.1.refs_1_, bf16[520,128]{1,0:T(8,128)(2,1)S(1)} %collective-permute-done.2.refs_2_, ...), custom_call_target="tpu_custom_call" | custom-call | tf_op jit(solution)/shard_map/near/pallas_call | solution.py:324
  38.5 0.1 collective-permute-start.3
  38.6 0.0 collective-permute-done.9
  38.6 0.1 fusion.1
  38.6 3.5 %collective-permute-start.10 = (bf16[128,1024]{1,0:T(8,128)(2,1)S(1)}, bf16[128,1024]{1,0:T(8,128)(2,1)S(1)}, u32[]{:S(2)}, u32[]{:S(2)}) collective-permute-start(bf16[128,1024]{1,0:T(8,128)(2,1)S(1)} %fusion.1), channel_id=1, source_target_pairs={{0,2},{1,3},{4,6},{5,7},{8,10},{9,11},{12,14},{13,15},{18,16},{19,... | collective-permute-start | bytes 786440 | tf_op jit(solution)/shard_map/ppermute | solution.py:355
  42.1 0.0 collective-permute-done.3
  42.1 0.1 fusion
  42.2 1.3 %collective-permute-start.4 = (bf16[128,1024]{1,0:T(8,128)(2,1)S(1)}, bf16[128,1024]{1,0:T(8,128)(2,1)S(1)}, u32[]{:S(2)}, u32[]{:S(2)}) collective-permute-start(bf16[128,1024]{1,0:T(8,128)(2,1)S(1)} %fusion), channel_id=1, source_target_pairs={{2,0},{3,1},{6,4},{7,5},{10,8},{11,9},{14,12},{15,13},{16,18},{17,... | collective-permute-start | bytes 786440 | tf_op jit(solution)/shard_map/ppermute | solution.py:355
  43.5 4.8 %collective-permute-done.10 = bf16[128,1024]{1,0:T(8,128)(2,1)S(1)} collective-permute-done((bf16[128,1024]{1,0:T(8,128)(2,1)S(1)}, bf16[128,1024]{1,0:T(8,128)(2,1)S(1)}, u32[]{:S(2)}, u32[]{:S(2)}) %collective-permute-start.10) | collective-permute-done | bytes 262176 | tf_op jit(solution)/shard_map/ppermute | solution.py:355
  48.3 4.2 %collective-permute-done.4 = bf16[128,1024]{1,0:T(8,128)(2,1)S(1)} collective-permute-done((bf16[128,1024]{1,0:T(8,128)(2,1)S(1)}, bf16[128,1024]{1,0:T(8,128)(2,1)S(1)}, u32[]{:S(2)}, u32[]{:S(2)}) %collective-permute-start.4) | collective-permute-done | bytes 262176 | tf_op jit(solution)/shard_map/ppermute | solution.py:355
  52.5 0.9 %select_convert_fusion = bf16[128,1024]{1,0:T(8,128)(2,1)} fusion(bf16[128,1024]{1,0:T(8,128)(2,1)S(1)} %collective-permute-done.10, bf16[128,1024]{1,0:T(8,128)(2,1)S(1)} %collective-permute-done.4, f32[128,1024]{1,0:T(8,128)S(1)} %get-tuple-element.27, bf16[128,1024]{1,0:T(8,128)(2,1)S(1)} %collective-permute-done.3, f32[128,1024]{1,0:T(8,128)S(1)} %get-tuple-element.31, ...), kind=kLoop, calls=%fused_computation | loop fusion | flops 1310720 | bytes 2359297 | tf_op jit(solution)/shard_map/convert_element_type | solution.py:370
Async XLA Ops:
  2.7 10.3 %collective-permute-start.5 = (bf16[520,128]{1,0:T(8,128)(2,1)S(1)}, bf16[520,128]{1,0:T(8,128)(2,1)S(1)}, u32[]{:S(2)}, u32[]{:S(2)}) collective-permute-start(bf16[520,128]{1,0:T(8,128)(2,1)S(1)} %get-tuple-element.29), channel_id=1, source_target_pairs={{0,28},{1,21},{2,30},{3,23},{4,24},{5,17},{6,26},{7,19},{8,20},{9,... | collective-permute-start | bytes 399368 | tf_op jit(solution)/shard_map/ppermute | solution.py:289
  8.7 6.9 %collective-permute-start.7 = (bf16[520,128]{1,0:T(8,128)(2,1)S(1)}, bf16[520,128]{1,0:T(8,128)(2,1)S(1)}, u32[]{:S(2)}, u32[]{:S(2)}) collective-permute-start(bf16[520,128]{1,0:T(8,128)(2,1)S(1)} %get-tuple-element.30), channel_id=1, source_target_pairs={{0,24},{1,17},{2,26},{3,19},{4,28},{5,21},{6,30},{7,23},{8,16},{9,... | collective-permute-start | bytes 399368 | tf_op jit(solution)/shard_map/ppermute | solution.py:289
  13.0 12.4 %collective-permute-start.6 = (bf16[520,128]{1,0:T(8,128)(2,1)S(1)}, bf16[520,128]{1,0:T(8,128)(2,1)S(1)}, u32[]{:S(2)}, u32[]{:S(2)}) collective-permute-start(bf16[520,128]{1,0:T(8,128)(2,1)S(1)} %collective-permute-done.5.refs_0_), channel_id=1, source_target_pairs={{0,1},{1,0},{2,3},{3,2},{4,5},{5,4},{6,7},{7,6},{8,9},{9,8},{10,11... | collective-permute-start | bytes 399368 | tf_op jit(solution)/shard_map/ppermute | solution.py:292
  15.7 9.8 %collective-permute-start.8 = (bf16[520,128]{1,0:T(8,128)(2,1)S(1)}, bf16[520,128]{1,0:T(8,128)(2,1)S(1)}, u32[]{:S(2)}, u32[]{:S(2)}) collective-permute-start(bf16[520,128]{1,0:T(8,128)(2,1)S(1)} %collective-permute-done.7.refs_2_), channel_id=1, source_target_pairs={{0,1},{1,0},{2,3},{3,2},{4,5},{5,4},{6,7},{7,6},{8,9},{9,8},{10,11... | collective-permute-start | bytes 399368 | tf_op jit(solution)/shard_map/ppermute | solution.py:292
  18.6 11.2 %collective-permute-start = (bf16[520,128]{1,0:T(8,128)(2,1)S(1)}, bf16[520,128]{1,0:T(8,128)(2,1)S(1)}, u32[]{:S(2)}, u32[]{:S(2)}) collective-permute-start(bf16[520,128]{1,0:T(8,128)(2,1)S(1)} %get-tuple-element.19), channel_id=1, source_target_pairs={{0,12},{1,5},{2,14},{3,7},{4,8},{5,1},{6,10},{7,3},{8,4},{9,13},{1... | collective-permute-start | bytes 399368 | tf_op jit(solution)/shard_map/ppermute | solution.py:289
  20.6 0.7 %copy-start.1 = (f32[1,32,8]{1,2,0:T(8,128)S(1)}, f32[1,32,8]{1,2,0:T(8,128)}, u32[]{:S(2)}) copy-start(f32[1,32,8]{1,2,0:T(8,128)} %param.17) | copy-start | bytes 3076
  21.3 4.1 %copy-start = (f32[1,1024]{1,0:T(1,128)S(1)}, f32[1,1024]{1,0:T(1,128)}, u32[]{:S(2)}) copy-start(f32[1,1024]{1,0:T(1,128)} %refs_4_.3) | copy-start | bytes 12292
  29.0 9.6 %collective-permute-start.9 = (bf16[128,1024]{1,0:T(8,128)(2,1)S(1)}, bf16[128,1024]{1,0:T(8,128)(2,1)S(1)}, u32[]{:S(2)}, u32[]{:S(2)}) collective-permute-start(bf16[128,1024]{1,0:T(8,128)(2,1)S(1)} %get-tuple-element.32), channel_id=1, source_target_pairs={{0,1},{1,0},{2,3},{3,2},{4,5},{5,4},{6,7},{7,6},{8,9},{9,8},{10,11... | collective-permute-start | bytes 786440 | tf_op jit(solution)/shard_map/ppermute | solution.py:292
  29.0 5.9 %collective-permute-start.2 = (bf16[520,128]{1,0:T(8,128)(2,1)S(1)}, bf16[520,128]{1,0:T(8,128)(2,1)S(1)}, u32[]{:S(2)}, u32[]{:S(2)}) collective-permute-start(bf16[520,128]{1,0:T(8,128)(2,1)S(1)} %get-tuple-element.20), channel_id=1, source_target_pairs={{0,8},{1,9},{2,10},{3,11},{4,12},{5,13},{6,14},{7,15},{8,0},{9,1},... | collective-permute-start | bytes 399368 | tf_op jit(solution)/shard_map/ppermute | solution.py:289
  29.7 5.2 %collective-permute-start.1 = (bf16[520,128]{1,0:T(8,128)(2,1)S(1)}, bf16[520,128]{1,0:T(8,128)(2,1)S(1)}, u32[]{:S(2)}, u32[]{:S(2)}) collective-permute-start(bf16[520,128]{1,0:T(8,128)(2,1)S(1)} %collective-permute-done.refs_0_), channel_id=1, source_target_pairs={{0,1},{1,0},{2,3},{3,2},{4,5},{5,4},{6,7},{7,6},{8,9},{9,8},{10,11... | collective-permute-start | bytes 399368 | tf_op jit(solution)/shard_map/ppermute | solution.py:292
  38.5 3.6 %collective-permute-start.3 = (bf16[128,1024]{1,0:T(8,128)(2,1)S(1)}, bf16[128,1024]{1,0:T(8,128)(2,1)S(1)}, u32[]{:S(2)}, u32[]{:S(2)}) collective-permute-start(bf16[128,1024]{1,0:T(8,128)(2,1)S(1)} %get-tuple-element.28), channel_id=1, source_target_pairs={{0,1},{1,0},{2,3},{3,2},{4,5},{5,4},{6,7},{7,6},{8,9},{9,8},{10,11... | collective-permute-start | bytes 786440 | tf_op jit(solution)/shard_map/ppermute | solution.py:292
  38.6 9.6 %collective-permute-start.10 = (bf16[128,1024]{1,0:T(8,128)(2,1)S(1)}, bf16[128,1024]{1,0:T(8,128)(2,1)S(1)}, u32[]{:S(2)}, u32[]{:S(2)}) collective-permute-start(bf16[128,1024]{1,0:T(8,128)(2,1)S(1)} %fusion.1), channel_id=1, source_target_pairs={{0,2},{1,3},{4,6},{5,7},{8,10},{9,11},{12,14},{13,15},{18,16},{19,... | collective-permute-start | bytes 786440 | tf_op jit(solution)/shard_map/ppermute | solution.py:355
  42.2 10.3 %collective-permute-start.4 = (bf16[128,1024]{1,0:T(8,128)(2,1)S(1)}, bf16[128,1024]{1,0:T(8,128)(2,1)S(1)}, u32[]{:S(2)}, u32[]{:S(2)}) collective-permute-start(bf16[128,1024]{1,0:T(8,128)(2,1)S(1)} %fusion), channel_id=1, source_target_pairs={{2,0},{3,1},{6,4},{7,5},{10,8},{11,9},{14,12},{15,13},{16,18},{17,... | collective-permute-start | bytes 786440 | tf_op jit(solution)/shard_map/ppermute | solution.py:355
where the time goes:
time: 53.6 us; the launch traced here: 53.4 us
  starting transfers between devices  19.5 us (36%)
  waiting for transfers between devices  18.3 us (34%)
  Pallas kernels  13.7 us (26%)
  other arithmetic  1.04 us (2%)
  local copies, waits for them, and re-layouts  0.69 us (1%)
    ppermute x4, waiting for transfers between devices, shift(): return lax.ppermute(value, ('tenant', 'tp'), moves)  9.27 us
    ppermute x4, starting transfers between devices, shift(): return lax.ppermute(value, ('tenant', 'tp'), moves)  9.03 us
    ppermute x2, waiting for transfers between devices, cross(): return lax.ppermute(value, ('tenant', 'tp'), moves)  8.99 us
    pallas_call x2, Pallas kernels, sublayer(): pl.pallas_call(functools.partial(sublayer_kernel, slots, is_far, cap, hal...  6.98 us
    ppermute x5, starting transfers between devices, swap(): return lax.ppermute(value, 'tp', [(t, t ^ 1) for t in range(tp)])  5.73 us
    ppermute x2, starting transfers between devices, cross(): return lax.ppermute(value, ('tenant', 'tp'), moves)  4.75 us
    pallas_call x1, Pallas kernels, per_device(): pl.pallas_call(functools.partial(prepare_kernel, bias_runs(extent, rel_bi...  4.1 us
    pallas_call x1, Pallas kernels, per_device(): pl.pallas_call(functools.partial(pack_kernel, rounds, cap), out_shape=[sl...  2.67 us
  transfers between devices with their start and end apart: 11, of which 4 were waited for; matrix products, arithmetic and copies ran while one was open for 0% of the time, Pallas kernels for 21%

commit v1 on v0

--- a/solution.py
+++ b/solution.py
@@ -68,24 +68,25 @@
     return pair[0] if pair[0] == pair[1] else jnp.where(core == 0, pair[0], pair[1])
 
 
-def pack_kernel(rounds, cap, tenant_hbm, length_hbm, tokens_hbm, *refs):
-    out_refs = refs[:-5]
-    select, tokens_ref, tenant_ref, length_ref, semaphore = refs[-5:]
+def pack_kernel(rounds, cap, runs, tenant_hbm, length_hbm, table_hbm, tokens_hbm, *refs):
+    out_refs, strip_ref = refs[:-7], refs[-7]
+    select, tokens_ref, tenant_ref, length_ref, table_ref, semaphore = refs[-6:]
     pairs = tenant_ref.shape[0]
     columns = tokens_ref.shape[1]
     tables = [
         pltpu.make_async_copy(tenant_hbm, tenant_ref, semaphore.at[0]),
         pltpu.make_async_copy(length_hbm, length_ref, semaphore.at[1]),
+        pltpu.make_async_copy(table_hbm, table_ref, semaphore.at[2]),
     ]
     for copy in tables:
         copy.start()
-    step = 2 * LANES
+    step = columns // 2
     fetches = []
     for i, at in enumerate(range(0, columns, step)):
         where = slice(at, at + step)
         fetches.append(
             pltpu.make_async_copy(
-                tokens_hbm.at[:, where], tokens_ref.at[:, where], semaphore.at[2 + i]
+                tokens_hbm.at[:, where], tokens_ref.at[:, where], semaphore.at[3 + i]
             )
         )
         fetches[-1].start()
@@ -119,6 +120,17 @@
         out_refs[slot][columns // LANES * cap :, :] = jnp.broadcast_to(
             seg.astype(jnp.float32), (SEG_ROWS, LANES)
         ).astype(jnp.bfloat16)
+    heads, band, double = strip_ref.shape
+    distance = (
+        lax.broadcasted_iota(jnp.int32, (band, double), 1)
+        - lax.broadcasted_iota(jnp.int32, (band, double), 0)
+        - double // 2
+    )
+    for head in range(heads):
+        strip = jnp.full(distance.shape, table_ref[head, runs[0][1]], jnp.float32)
+        for start, bucket in runs[1:]:
+            strip = jnp.where(distance >= start, table_ref[head, bucket], strip)
+        strip_ref[head] = strip
     for fetch, at in zip(fetches, range(0, columns, step)):
         fetch.wait()
         packed = jnp.dot(
@@ -132,46 +144,37 @@
                 ]
 
 
-def prepare_kernel(runs, table_ref, *refs):
-    count = (len(refs) - 2) // 2
-    sources, bias_ref, targets, semaphore = refs[:count], refs[count], refs[count + 1 : -1], refs[-1]
-    copies = []
-    for i, (source, target) in enumerate(zip(sources, targets)):
-        copies.append(pltpu.make_async_copy(source, target, semaphore.at[i]))
-        copies[-1].start()
-    heads, extent = bias_ref.shape[0], bias_ref.shape[1]
-    distance = lax.broadcasted_iota(jnp.int32, (extent, extent), 1) - lax.broadcasted_iota(
-        jnp.int32, (extent, extent), 0
-    )
+def bias_kernel(strip_ref, bias_ref):
+    heads, band, double = strip_ref.shape
+    extent = double // 2
     for head in range(heads):
-        value = jnp.full((extent, extent), table_ref[head, runs[0][1]], jnp.float32)
-        for start, bucket in runs[1:]:
-            value = jnp.where(distance >= start, table_ref[head, bucket], value)
-        bias_ref[head] = value
-    for copy in copies:
-        copy.wait()
-
-
-def sublayer_kernel(slots, far, cap, slot_count, *refs):
-    slot_refs = refs[:slot_count]
-    gain_ref, wq_ref, wk_ref, wv_ref, wo_ref, bias_ref = refs[slot_count : slot_count + 6]
-    send_ref, keep_ref, x, seg, normed, q, k, v, context, score, top, weight = refs[
-        slot_count + 6 :
+        strip = strip_ref[head]
+        for row in range(0, extent, band):
+            turned = pltpu.roll(strip, (row - extent) % double, 1)
+            bias_ref[head, row : row + band] = turned[:, :extent]
+
+
+def sublayer_kernel(slots, far, half, cap, *refs):
+    count, split = len(slots), half // 2
+    slot_refs = refs[:count]
+    gain_ref, wq_ref, wk_ref, wv_ref, wo_ref, bias_ref, send_ref, keep_ref = refs[
+        count : count + 8
     ]
-    half, split = slot_count, slot_count // 2
+    x, seg, normed, q, k, v, context, score, top, weight = refs[count + 8 :]
     width = x.shape[1]
+    part = count // 2
     me = lax.axis_index("tenant")
     t = lax.axis_index("tp")
     core, outer = lax.rem(t, 2), t // 2
     for ref, pair in zip(slot_refs, slots):
-        slot = lax.bitwise_and(lax.bitwise_xor(me, jnp.int32(pick(core, pair))), half - 1)
-        at = lax.bitwise_xor(slot, (1 - core) * split)
+        mine = lax.rem(lax.bitwise_xor(me, jnp.int32(pick(core, pair))) // split, 2) == core
+        at = jnp.where(mine, part, 0) + (pair[0] % part)
         for c in range(width // LANES):
             x[pl.ds(pl.multiple_of(at * cap, cap), cap), c * LANES : (c + 1) * LANES] = ref[
                 c * cap : (c + 1) * cap, :
             ]
         seg[at] = ref[width // LANES * cap :, :].astype(jnp.float32)
-    total = half * cap
+    total = count * cap
     step = min(BLOCK, total)
     inner = min(LANES, total)
     side = inner // cap
@@ -233,16 +236,38 @@
                     alive, both[:, :size] * (1.0 / both[:, size:]), 0.0
                 ).astype(jnp.bfloat16)
         partial = jnp.dot(context[...], wo_ref[...], preferred_element_type=jnp.float32)
-        for at in range(0, step, split * cap) if step > split * cap else (0,):
-            size_out = min(step, split * cap)
+        size_out = min(step, part * cap)
+        for at in range(0, step, size_out):
             row = base + at
             piece = partial[at : at + size_out]
-            if row < split * cap:
+            if row < part * cap:
                 send_ref[row : row + size_out] = piece.astype(jnp.bfloat16)
             else:
-                keep_ref[row - split * cap : row - split * cap + size_out] = (
+                keep_ref[row - part * cap : row - part * cap + size_out] = (
                     piece + scale * x[row : row + size_out].astype(jnp.float32)
                 )
+
+
+def join_kernel(relative, near_keep, near_got, far_keep, far_got, own_ref, send_ref):
+    cap = far_keep.shape[0]
+    rows = slice(relative * cap, (relative + 1) * cap)
+    half = lax.axis_size("tenant") // 2
+    owner = lax.axis_index("tenant") // half == lax.axis_index("tp") // 2
+    near = near_keep[rows] + near_got[rows].astype(jnp.float32)
+    far = far_keep[...] + far_got[...].astype(jnp.float32)
+    own_ref[...] = jnp.where(owner, near, far)
+    send_ref[...] = jnp.where(owner, far, near).astype(jnp.bfloat16)
+
+
+def finish_kernel(cap, *refs):
+    pieces = len(refs) // 2
+    own_refs, other_refs, out_ref = refs[:pieces], refs[pieces:-1], refs[-1]
+    me = lax.axis_index("tenant")
+    for i in range(pieces):
+        at = lax.bitwise_xor(lax.rem(me, pieces), pieces - 1 - i)
+        out_ref[pl.ds(pl.multiple_of(at * cap, cap), cap), :] = (
+            own_refs[i][...] + other_refs[i][...].astype(jnp.float32)
+        ).astype(jnp.bfloat16)
 
 
 def per_device(
@@ -261,25 +286,39 @@
     pairs, cap, width = src_tokens.shape
     half, split = tenants // 2, tenants // 4
     far, near = plan(tenants)
-    rounds = far + near + [(0, 0)]
+    rounds = near + far + [(0, 0)]
     slot_shape = pltpu.VMEM((width // LANES * cap + SEG_ROWS, LANES), jnp.bfloat16)
-    packed = pl.pallas_call(
-        functools.partial(pack_kernel, rounds, cap),
-        out_shape=[slot_shape] * len(rounds),
-        in_specs=[HBM, HBM, HBM],
-        out_specs=[VMEM] * len(rounds),
+    buckets, heads = rel_bias.shape[1:]
+    extent = min(LANES, half * cap)
+    *packed, strips = pl.pallas_call(
+        functools.partial(pack_kernel, rounds, cap, bias_runs(extent, buckets)),
+        out_shape=[slot_shape] * len(rounds)
+        + [pltpu.VMEM((heads, 8, 2 * extent), jnp.float32)],
+        in_specs=[HBM] * 4,
+        out_specs=[VMEM] * (len(rounds) + 1),
         scratch_shapes=[
             pltpu.VMEM((len(rounds) * cap, pairs * cap), jnp.bfloat16),
             pltpu.VMEM((pairs * cap, width), jnp.bfloat16),
             pltpu.SMEM((pairs,), jnp.int32),
             pltpu.SMEM((pairs,), jnp.int32),
-            pltpu.SemaphoreType.DMA((2 + width // (2 * LANES),)),
+            pltpu.SMEM((heads, buckets), jnp.float32),
+            pltpu.SemaphoreType.DMA((5,)),
         ],
         compiler_params=pltpu.CompilerParams(
             vmem_limit_bytes=2 * MIB + 2 * pairs * cap * (width + (len(rounds) + 1) * cap)
         ),
         name="pack",
-    )(*map(in_hbm, (pair_tenant, pair_length, src_tokens.reshape(pairs * cap, width))))
+    )(
+        *map(
+            in_hbm,
+            (
+                pair_tenant,
+                pair_length,
+                rel_bias[0].T,
+                src_tokens.reshape(pairs * cap, width),
+            ),
+        )
+    )
 
     def shift(value, pair):
         moves = []
@@ -295,19 +334,18 @@
     for value, pair in zip(packed, rounds[:-1]):
         arrived.append(shift(value, pair))
 
-    heads = rel_bias.shape[2]
-    extent = min(LANES, half * cap)
-    raw = [w[0] for w in (w_query, w_key, w_value, w_out)]
-    bias, *weights = pl.pallas_call(
-        functools.partial(prepare_kernel, bias_runs(extent, rel_bias.shape[1])),
-        out_shape=[pltpu.VMEM((heads, extent, extent), jnp.float32)]
-        + [pltpu.VMEM(w.shape, w.dtype) for w in raw],
-        in_specs=[SMEM] + [HBM] * len(raw),
-        out_specs=[VMEM] * (1 + len(raw)),
-        scratch_shapes=[pltpu.SemaphoreType.DMA((len(raw),))],
+    weights = [w[0] for w in (w_query, w_key, w_value, w_out)]
+    bias = pl.pallas_call(
+        bias_kernel,
+        out_shape=pltpu.VMEM((heads, extent, extent), jnp.float32),
+        in_specs=[VMEM],
+        out_specs=VMEM,
         compiler_params=pltpu.CompilerParams(vmem_limit_bytes=4 * MIB),
+        cost_estimate=pl.CostEstimate(
+            flops=10**10, bytes_accessed=0, transcendentals=0
+        ),
         name="prepare",
-    )(rel_bias[0].T, *map(in_hbm, raw))
+    )(in_vmem(strips))
 
     def sublayer(rounds_here, values, is_far):
         slots, arrays = [], []
@@ -317,57 +355,66 @@
             if pair[0] != pair[1]:
                 slots.append(pair[::-1])
                 arrays.append(swap(value))
-        total = half * cap
+        count = len(slots)
+        total = count * cap
         step = min(BLOCK, total)
+        inner = min(LANES, total)
         own = w_query.shape[2]
-        vmem = 8 * MIB + 4 * total * width
-        return pl.pallas_call(
-            functools.partial(sublayer_kernel, slots, is_far, cap, half),
+        send, keep = pl.pallas_call(
+            functools.partial(sublayer_kernel, slots, is_far, half, cap),
             out_shape=[
-                pltpu.VMEM((split * cap, width), jnp.bfloat16),
-                pltpu.VMEM((split * cap, width), jnp.float32),
+                pltpu.VMEM((total // 2, width), jnp.bfloat16),
+                pltpu.VMEM((total // 2, width), jnp.float32),
             ],
-            in_specs=[VMEM] * (half + 6),
-            out_specs=[VMEM, VMEM],
+            in_specs=[VMEM] * (count + 6),
+            out_specs=[VMEM] * 2,
             scratch_shapes=[
                 pltpu.VMEM((total, width), jnp.bfloat16),
-                pltpu.VMEM((half, SEG_ROWS, LANES), jnp.float32),
+                pltpu.VMEM((count, SEG_ROWS, LANES), jnp.float32),
                 pltpu.VMEM((step, width), jnp.bfloat16),
                 pltpu.VMEM((step, own), jnp.bfloat16),
                 pltpu.VMEM((step, own), jnp.bfloat16),
                 pltpu.VMEM((step, own), jnp.bfloat16),
                 pltpu.VMEM((step, own), jnp.bfloat16),
-                pltpu.VMEM((heads, extent, extent), jnp.float32),
-                pltpu.VMEM((heads, extent, extent), jnp.float32),
-                pltpu.VMEM((heads, extent, extent), jnp.bfloat16),
+                pltpu.VMEM((heads, inner, inner), jnp.float32),
+                pltpu.VMEM((heads, inner, inner), jnp.float32),
+                pltpu.VMEM((heads, inner, inner), jnp.bfloat16),
             ],
-            compiler_params=pltpu.CompilerParams(vmem_limit_bytes=vmem),
-            name="far" if is_far else "near",
-        )(*[in_vmem(value) for value in arrays], norm_gain, *map(in_vmem, weights), in_vmem(bias))
-
-    def cross(value, is_far):
-        moves = []
-        for u in range(tenants):
-            for t in range(tp):
-                owner = (u // half == t // 2) != is_far
-                if not owner:
-                    moves.append((u * tp + t, u * tp + (t ^ 2)))
-        return lax.ppermute(value, ("tenant", "tp"), moves)
-
-    def reduced(rounds_here, values, is_far):
-        send, keep = sublayer(rounds_here, values, is_far)
-        other = swap(send)
-        pair_sum = keep + other.astype(jnp.float32)
-        return pair_sum, cross(pair_sum.astype(jnp.bfloat16), is_far)
-
-    near_sum, near_other = reduced(near + [(0, 0)], arrived[len(far) :] + [packed[-1]], False)
-    far_sum, far_other = reduced(far, arrived[: len(far)], True)
-    owner = lax.axis_index("tenant") // half == lax.axis_index("tp") // 2
-    return jnp.where(
-        owner,
-        near_sum + near_other.astype(jnp.float32),
-        far_sum + far_other.astype(jnp.float32),
-    ).astype(jnp.bfloat16)
+            compiler_params=pltpu.CompilerParams(
+                vmem_limit_bytes=6 * MIB + 4 * total * width
+            ),
+        )(
+            *map(in_vmem, arrays),
+            norm_gain,
+            *map(in_vmem, weights),
+            in_vmem(bias),
+        )
+        return keep, swap(send)
+
+    near_sums = sublayer(near + [(0, 0)], arrived[: len(near)] + [packed[-1]], False)
+    own, others = [], []
+    for i, pair in enumerate(far):
+        far_sums = sublayer([pair], [arrived[len(near) + i]], True)
+        kept, send = pl.pallas_call(
+            functools.partial(join_kernel, split - 1 - i),
+            out_shape=[
+                pltpu.VMEM((cap, width), jnp.float32),
+                pltpu.VMEM((cap, width), jnp.bfloat16),
+            ],
+            in_specs=[VMEM] * 4,
+            out_specs=[VMEM] * 2,
+            compiler_params=pltpu.CompilerParams(vmem_limit_bytes=MIB),
+        )(*map(in_vmem, (*near_sums, *far_sums)))
+        others.append(lax.ppermute(send, "tp", [(t, t ^ 2) for t in range(tp)]))
+        own.append(kept)
+    return pl.pallas_call(
+        functools.partial(finish_kernel, cap),
+        out_shape=jax.ShapeDtypeStruct((split * cap, width), jnp.bfloat16),
+        in_specs=[VMEM] * (2 * split),
+        out_specs=VMEM,
+        compiler_params=pltpu.CompilerParams(vmem_limit_bytes=MIB + 4 * split * cap * width),
+        name="finish",
+    )(*map(in_vmem, (*own, *others)))
 
 
 def solution(mesh):

time: 53.6 us -> 39.6 us (0.74)
  starting transfers between devices: 19.5 us -> 12 us
  waiting for transfers between devices: 18.3 us -> 13.6 us
  Pallas kernels: 13.7 us -> 10.6 us
  local copies, waits for them, and re-layouts: 0.69 us -> 3.11 us
  other arithmetic: 1.04 us -> 0 us
    ppermute x5 -> x6, starting transfers between devices: 5.73 us -> 1.31 us  [swap(): return lax.ppermute(value, 'tp', [(t, t ^ 1) for t in range(tp)])]
    ppermute x2, waiting for transfers between devices: 8.99 us -> 5.84 us  [per_device(): others.append(lax.ppermute(send, 'tp', [(t, t ^ 2) for t in range(tp)]))]
    pallas_call x4 -> x8, Pallas kernels: 13.7 us -> 10.6 us  [the longest x3 7.38 us: sublayer(): pl.pallas_call(functools.partial(sublayer_kernel, slots, is_far, half, ca...]
    unnamed x4 -> x10, local copies, waits for them, and re-layouts: 0.69 us -> 3.11 us
    ppermute x2, starting transfers between devices: 4.75 us -> 2.83 us  [per_device(): others.append(lax.ppermute(send, 'tp', [(t, t ^ 2) for t in range(tp)]))]
    ppermute x4, waiting for transfers between devices: 9.27 us -> 7.78 us  [shift(): return lax.ppermute(value, ('tenant', 'tp'), moves)]
    ppermute x4, starting transfers between devices: 9.03 us -> 7.84 us  [shift(): return lax.ppermute(value, ('tenant', 'tp'), moves)]
    convert_element_type x3 -> x0, other arithmetic: 1.04 us -> none  [the longest x1 0.93 us: per_device(): return jnp.where(owner, near_sum + near_other.astype(jnp.float32), far_su...]
  transfers between devices with their start and end apart: 11 -> 12, of which waited for: 4 -> 5; matrix products, arithmetic and copies ran while one was open for 0% -> 0% of each run, Pallas kernels for 21% -> 20%
where the time goes in v1:
time: 39.6 us; the launch traced here: 39.5 us
  waiting for transfers between devices  13.6 us (34%)
  starting transfers between devices  12 us (30%)
  Pallas kernels  10.6 us (27%)
  local copies, waits for them, and re-layouts  3.11 us (8%)
    ppermute x4, starting transfers between devices, shift(): return lax.ppermute(value, ('tenant', 'tp'), moves)  7.84 us
    ppermute x4, waiting for transfers between devices, shift(): return lax.ppermute(value, ('tenant', 'tp'), moves)  7.78 us
    pallas_call x3, Pallas kernels, sublayer(): pl.pallas_call(functools.partial(sublayer_kernel, slots, is_far, half, ca...  7.38 us
    ppermute x2, waiting for transfers between devices, per_device(): others.append(lax.ppermute(send, 'tp', [(t, t ^ 2) for t in range(tp)]))  5.84 us
    unnamed x10, local copies, waits for them, and re-layouts  3.11 us
    ppermute x2, starting transfers between devices, per_device(): others.append(lax.ppermute(send, 'tp', [(t, t ^ 2) for t in range(tp)]))  2.83 us
    pallas_call x1, Pallas kernels, per_device(): pl.pallas_call(functools.partial(pack_kernel, rounds, cap, bias_runs(exte...  2.02 us
    ppermute x6, starting transfers between devices, swap(): return lax.ppermute(value, 'tp', [(t, t ^ 1) for t in range(tp)])  1.31 us
  transfers between devices with their start and end apart: 12, of which 5 were waited for; matrix products, arithmetic and copies ran while one was open for 0% of the time, Pallas kernels for 20%

profile of v1, /device:TPU:0, one launch (start us, length us, event | category | flops | bytes accessed | tf_op | source)
XLA Modules:
  0.0 39.5 jit_solution(1715148859770317060)
XLA Ops:
  0.0 2.0 %pack.1 = (bf16[520,128]{1,0:T(8,128)(2,1)S(1)}, bf16[520,128]{1,0:T(8,128)(2,1)S(1)}, bf16[520,128]{1,0:T(8,128)(2,1)S(1)}, bf16[520,128]{1,0:T(8,128)(2,1)S(1)...) custom-call(s32[12]{0:T(128)} %tenant_hbm.1, s32[12]{0:T(128)} %length_hbm.1, f32[8,32]{1,0:T(8,128)} %bitcast.21, ...), custom_call_target="tpu_custom_call" | custom-call | tf_op jit(solution)/shard_map/pack/pallas_call | solution.py:293
  2.0 4.0 %collective-permute-start = (bf16[520,128]{1,0:T(8,128)(2,1)S(1)}, bf16[520,128]{1,0:T(8,128)(2,1)S(1)}, u32[]{:S(2)}, u32[]{:S(2)}) collective-permute-start(bf16[520,128]{1,0:T(8,128)(2,1)S(1)} %get-tuple-element.21), channel_id=1, source_target_pairs={{0,12},{1,5},{2,14},{3,7},{4,8},{5,1},{6,10},{7,3},{8,4},{9,13},{1... | collective-permute-start | bytes 399368 | tf_op jit(solution)/shard_map/ppermute | solution.py:328
  6.1 2.5 %collective-permute-start.7 = (bf16[520,128]{1,0:T(8,128)(2,1)S(1)}, bf16[520,128]{1,0:T(8,128)(2,1)S(1)}, u32[]{:S(2)}, u32[]{:S(2)}) collective-permute-start(bf16[520,128]{1,0:T(8,128)(2,1)S(1)} %get-tuple-element.31), channel_id=1, source_target_pairs={{0,24},{1,17},{2,26},{3,19},{4,28},{5,21},{6,30},{7,23},{8,16},{9,... | collective-permute-start | bytes 399368 | tf_op jit(solution)/shard_map/ppermute | solution.py:328
  8.6 1.3 %collective-permute-start.4 = (bf16[520,128]{1,0:T(8,128)(2,1)S(1)}, bf16[520,128]{1,0:T(8,128)(2,1)S(1)}, u32[]{:S(2)}, u32[]{:S(2)}) collective-permute-start(bf16[520,128]{1,0:T(8,128)(2,1)S(1)} %get-tuple-element.27), channel_id=1, source_target_pairs={{0,28},{1,21},{2,30},{3,23},{4,24},{5,17},{6,26},{7,19},{8,20},{9,... | collective-permute-start | bytes 399368 | tf_op jit(solution)/shard_map/ppermute | solution.py:328
  9.9 0.0 collective-permute-start.2
  9.9 0.3 collective-permute-done.refs_0_
  10.2 0.0 collective-permute-start.1
  10.2 5.3 %collective-permute-done.7.refs_0_ = bf16[520,128]{1,0:T(8,128)(2,1)S(1)} collective-permute-done((bf16[520,128]{1,0:T(8,128)(2,1)S(1)}, bf16[520,128]{1,0:T(8,128)(2,1)S(1)}, u32[]{:S(2)}, u32[]{:S(2)}) %collective-permute-start.7) | collective-permute-done | bytes 133152 | tf_op jit(solution)/shard_map/ppermute | solution.py:328
  15.5 0.0 collective-permute-start.8
  15.5 2.2 %collective-permute-done.4.refs_0_ = bf16[520,128]{1,0:T(8,128)(2,1)S(1)} collective-permute-done((bf16[520,128]{1,0:T(8,128)(2,1)S(1)}, bf16[520,128]{1,0:T(8,128)(2,1)S(1)}, u32[]{:S(2)}, u32[]{:S(2)}) %collective-permute-start.4) | collective-permute-done | bytes 133152 | tf_op jit(solution)/shard_map/ppermute | solution.py:328
  17.7 0.6 %collective-permute-start.5 = (bf16[520,128]{1,0:T(8,128)(2,1)S(1)}, bf16[520,128]{1,0:T(8,128)(2,1)S(1)}, u32[]{:S(2)}, u32[]{:S(2)}) collective-permute-start(bf16[520,128]{1,0:T(8,128)(2,1)S(1)} %collective-permute-done.4.refs_0_), channel_id=1, source_target_pairs={{0,1},{1,0},{2,3},{3,2},{4,5},{5,4},{6,7},{7,6},{8,9},{9,8},{10,11... | collective-permute-start | bytes 399368 | tf_op jit(solution)/shard_map/ppermute | solution.py:331
  18.3 0.0 copy-start
  18.3 0.0 copy-start.1
  18.3 0.0 copy-start.2
  18.3 0.0 copy-start.3
  18.3 0.0 copy-start.4
  18.3 0.3 prepare.1.refs_9_.refs_7_
  18.6 0.0 collective-permute-done.2.refs_2_
  18.6 0.0 collective-permute-done.1.refs_1_
  18.6 1.2 %copy-done = bf16[1,1024,1024]{2,1,0:T(8,128)(2,1)S(1)} copy-done((bf16[1,1024,1024]{2,1,0:T(8,128)(2,1)S(1)}, bf16[1,1024,1024]{2,1,0:T(8,128)(2,1)}, u32[]{:S(2)}) %copy-start) | copy-done | bytes 2097176
  19.9 0.6 %copy-done.1 = bf16[1,1024,1024]{2,1,0:T(8,128)(2,1)S(1)} copy-done((bf16[1,1024,1024]{2,1,0:T(8,128)(2,1)S(1)}, bf16[1,1024,1024]{2,1,0:T(8,128)(2,1)}, u32[]{:S(2)}) %copy-start.1) | copy-done | bytes 2097176
  20.5 0.6 %copy-done.2 = bf16[1,1024,1024]{2,1,0:T(8,128)(2,1)S(1)} copy-done((bf16[1,1024,1024]{2,1,0:T(8,128)(2,1)S(1)}, bf16[1,1024,1024]{2,1,0:T(8,128)(2,1)}, u32[]{:S(2)}) %copy-start.2) | copy-done | bytes 2097176
  21.1 0.6 %copy-done.3 = bf16[1,1024,1024]{2,1,0:T(8,128)(2,1)S(1)} copy-done((bf16[1,1024,1024]{2,1,0:T(8,128)(2,1)S(1)}, bf16[1,1024,1024]{2,1,0:T(8,128)(2,1)}, u32[]{:S(2)}) %copy-start.3) | copy-done | bytes 2097176
  21.7 0.0 copy-done.4
  21.7 3.5 %shard_map.91 = (bf16[128,1024]{1,0:T(8,128)(2,1)S(1)}, f32[128,1024]{1,0:T(8,128)S(1)}) custom-call(bf16[520,128]{1,0:T(8,128)(2,1)S(1)} %collective-permute-done.refs_0_, bf16[520,128]{1,0:T(8,128)(2,1)S(1)} %collective-permute-done.1.refs_1_, bf16[520,128]{1,0:T(8,128)(2,1)S(1)} %collective-permute-done.2.refs_2_, ...), custom_call_target="tpu_custom_call" | custom-call | tf_op jit(solution)/shard_map/pallas_call | solution.py:363
  25.3 0.1 collective-permute-start.3
  25.3 0.0 collective-permute-done.8.refs_1_
  25.4 1.9 %shard_map.94 = (bf16[64,1024]{1,0:T(8,128)(2,1)S(1)}, f32[64,1024]{1,0:T(8,128)S(1)}) custom-call(bf16[520,128]{1,0:T(8,128)(2,1)S(1)} %collective-permute-done.7.refs_0_, bf16[520,128]{1,0:T(8,128)(2,1)S(1)} %collective-permute-done.8.refs_1_, f32[1,1024]{1,0:T(1,128)S(1)} %copy-done.4, bf16[1024,1024]{1,0:T(8,128)(2,1)S(1)} %bitcast.9, ...), custom_call_target="tpu_custom_call" | custom-call | tf_op jit(solution)/shard_map/pallas_call | solution.py:363
  27.3 0.6 %collective-permute-start.9 = (bf16[64,1024]{1,0:T(8,128)(2,1)S(1)}, bf16[64,1024]{1,0:T(8,128)(2,1)S(1)}, u32[]{:S(2)}, u32[]{:S(2)}) collective-permute-start(bf16[64,1024]{1,0:T(8,128)(2,1)S(1)} %get-tuple-element.33), channel_id=1, source_target_pairs={{0,1},{1,0},{2,3},{3,2},{4,5},{5,4},{6,7},{7,6},{8,9},{9,8},{10,11... | collective-permute-start | bytes 393224 | tf_op jit(solution)/shard_map/ppermute | solution.py:331
  27.8 0.0 collective-permute-done.5.refs_1_
  27.8 1.9 %shard_map.92 = (bf16[64,1024]{1,0:T(8,128)(2,1)S(1)}, f32[64,1024]{1,0:T(8,128)S(1)}) custom-call(bf16[520,128]{1,0:T(8,128)(2,1)S(1)} %collective-permute-done.4.refs_0_, bf16[520,128]{1,0:T(8,128)(2,1)S(1)} %collective-permute-done.5.refs_1_, f32[1,1024]{1,0:T(1,128)S(1)} %copy-done.4, bf16[1024,1024]{1,0:T(8,128)(2,1)S(1)} %bitcast.10, ...), custom_call_target="tpu_custom_call" | custom-call | tf_op jit(solution)/shard_map/pallas_call | solution.py:363
  29.8 0.1 collective-permute-start.6
  29.9 0.0 collective-permute-done.9.far_got
  29.9 0.0 collective-permute-done.3.near_got
  29.9 0.1 shard_map.95
  30.0 1.6 %collective-permute-start.11 = (bf16[64,1024]{1,0:T(8,128)(2,1)S(1)}, bf16[64,1024]{1,0:T(8,128)(2,1)S(1)}, u32[]{:S(2)}, u32[]{:S(2)}) collective-permute-start(bf16[64,1024]{1,0:T(8,128)(2,1)S(1)} %get-tuple-element.36), channel_id=1, source_target_pairs={{0,2},{1,3},{2,0},{3,1},{4,6},{5,7},{6,4},{7,5},{8,10},{9,11},{10,... | collective-permute-start | bytes 393224 | tf_op jit(solution)/shard_map/ppermute | solution.py:408
  31.6 0.0 collective-permute-done.6.far_got
  31.6 0.1 shard_map.93
  31.7 1.2 %collective-permute-start.10 = (bf16[64,1024]{1,0:T(8,128)(2,1)S(1)}, bf16[64,1024]{1,0:T(8,128)(2,1)S(1)}, u32[]{:S(2)}, u32[]{:S(2)}) collective-permute-start(bf16[64,1024]{1,0:T(8,128)(2,1)S(1)} %get-tuple-element.35), channel_id=1, source_target_pairs={{0,2},{1,3},{2,0},{3,1},{4,6},{5,7},{6,4},{7,5},{8,10},{9,11},{10,... | collective-permute-start | bytes 393224 | tf_op jit(solution)/shard_map/ppermute | solution.py:408
  32.9 3.5 %collective-permute-done.11.refs_3_ = bf16[64,1024]{1,0:T(8,128)(2,1)S(1)} collective-permute-done((bf16[64,1024]{1,0:T(8,128)(2,1)S(1)}, bf16[64,1024]{1,0:T(8,128)(2,1)S(1)}, u32[]{:S(2)}, u32[]{:S(2)}) %collective-permute-start.11) | collective-permute-done | bytes 131104 | tf_op jit(solution)/shard_map/ppermute | solution.py:408
  36.4 2.3 %collective-permute-done.10.refs_2_ = bf16[64,1024]{1,0:T(8,128)(2,1)S(1)} collective-permute-done((bf16[64,1024]{1,0:T(8,128)(2,1)S(1)}, bf16[64,1024]{1,0:T(8,128)(2,1)S(1)}, u32[]{:S(2)}, u32[]{:S(2)}) %collective-permute-start.10) | collective-permute-done | bytes 131104 | tf_op jit(solution)/shard_map/ppermute | solution.py:408
  38.7 0.7 %finish.1 = bf16[128,1024]{1,0:T(8,128)(2,1)} custom-call(f32[64,1024]{1,0:T(8,128)S(1)} %get-tuple-element.30.refs_0_, f32[64,1024]{1,0:T(8,128)S(1)} %get-tuple-element.34.refs_1_, bf16[64,1024]{1,0:T(8,128)(2,1)S(1)} %collective-permute-done.10.refs_2_, bf16[64,1024]{1,0:T(8,128)(2,1)S(1)} %collective-permute-done.11.refs_3_), custom_call_target="tpu_custom_call" | custom-call | tf_op jit(solution)/shard_map/finish/pallas_call | solution.py:410
Async XLA Ops:
  2.0 8.1 %collective-permute-start = (bf16[520,128]{1,0:T(8,128)(2,1)S(1)}, bf16[520,128]{1,0:T(8,128)(2,1)S(1)}, u32[]{:S(2)}, u32[]{:S(2)}) collective-permute-start(bf16[520,128]{1,0:T(8,128)(2,1)S(1)} %get-tuple-element.21), channel_id=1, source_target_pairs={{0,12},{1,5},{2,14},{3,7},{4,8},{5,1},{6,10},{7,3},{8,4},{9,13},{1... | collective-permute-start | bytes 399368 | tf_op jit(solution)/shard_map/ppermute | solution.py:328
  6.1 9.4 %collective-permute-start.7 = (bf16[520,128]{1,0:T(8,128)(2,1)S(1)}, bf16[520,128]{1,0:T(8,128)(2,1)S(1)}, u32[]{:S(2)}, u32[]{:S(2)}) collective-permute-start(bf16[520,128]{1,0:T(8,128)(2,1)S(1)} %get-tuple-element.31), channel_id=1, source_target_pairs={{0,24},{1,17},{2,26},{3,19},{4,28},{5,21},{6,30},{7,23},{8,16},{9,... | collective-permute-start | bytes 399368 | tf_op jit(solution)/shard_map/ppermute | solution.py:328
  8.6 9.1 %collective-permute-start.4 = (bf16[520,128]{1,0:T(8,128)(2,1)S(1)}, bf16[520,128]{1,0:T(8,128)(2,1)S(1)}, u32[]{:S(2)}, u32[]{:S(2)}) collective-permute-start(bf16[520,128]{1,0:T(8,128)(2,1)S(1)} %get-tuple-element.27), channel_id=1, source_target_pairs={{0,28},{1,21},{2,30},{3,23},{4,24},{5,17},{6,26},{7,19},{8,20},{9,... | collective-permute-start | bytes 399368 | tf_op jit(solution)/shard_map/ppermute | solution.py:328
  9.9 8.7 %collective-permute-start.2 = (bf16[520,128]{1,0:T(8,128)(2,1)S(1)}, bf16[520,128]{1,0:T(8,128)(2,1)S(1)}, u32[]{:S(2)}, u32[]{:S(2)}) collective-permute-start(bf16[520,128]{1,0:T(8,128)(2,1)S(1)} %get-tuple-element.22), channel_id=1, source_target_pairs={{0,8},{1,9},{2,10},{3,11},{4,12},{5,13},{6,14},{7,15},{8,0},{9,1},... | collective-permute-start | bytes 399368 | tf_op jit(solution)/shard_map/ppermute | solution.py:328
  10.2 8.5 %collective-permute-start.1 = (bf16[520,128]{1,0:T(8,128)(2,1)S(1)}, bf16[520,128]{1,0:T(8,128)(2,1)S(1)}, u32[]{:S(2)}, u32[]{:S(2)}) collective-permute-start(bf16[520,128]{1,0:T(8,128)(2,1)S(1)} %collective-permute-done.refs_0_), channel_id=1, source_target_pairs={{0,1},{1,0},{2,3},{3,2},{4,5},{5,4},{6,7},{7,6},{8,9},{9,8},{10,11... | collective-permute-start | bytes 399368 | tf_op jit(solution)/shard_map/ppermute | solution.py:331
  15.5 9.9 %collective-permute-start.8 = (bf16[520,128]{1,0:T(8,128)(2,1)S(1)}, bf16[520,128]{1,0:T(8,128)(2,1)S(1)}, u32[]{:S(2)}, u32[]{:S(2)}) collective-permute-start(bf16[520,128]{1,0:T(8,128)(2,1)S(1)} %collective-permute-done.7.refs_0_), channel_id=1, source_target_pairs={{0,1},{1,0},{2,3},{3,2},{4,5},{5,4},{6,7},{7,6},{8,9},{9,8},{10,11... | collective-permute-start | bytes 399368 | tf_op jit(solution)/shard_map/ppermute | solution.py:331
  17.7 10.2 %collective-permute-start.5 = (bf16[520,128]{1,0:T(8,128)(2,1)S(1)}, bf16[520,128]{1,0:T(8,128)(2,1)S(1)}, u32[]{:S(2)}, u32[]{:S(2)}) collective-permute-start(bf16[520,128]{1,0:T(8,128)(2,1)S(1)} %collective-permute-done.4.refs_0_), channel_id=1, source_target_pairs={{0,1},{1,0},{2,3},{3,2},{4,5},{5,4},{6,7},{7,6},{8,9},{9,8},{10,11... | collective-permute-start | bytes 399368 | tf_op jit(solution)/shard_map/ppermute | solution.py:331
  18.3 1.6 %copy-start = (bf16[1,1024,1024]{2,1,0:T(8,128)(2,1)S(1)}, bf16[1,1024,1024]{2,1,0:T(8,128)(2,1)}, u32[]{:S(2)}) copy-start(bf16[1,1024,1024]{2,1,0:T(8,128)(2,1)} %param.13) | copy-start | bytes 6291460
  18.3 2.2 %copy-start.1 = (bf16[1,1024,1024]{2,1,0:T(8,128)(2,1)S(1)}, bf16[1,1024,1024]{2,1,0:T(8,128)(2,1)}, u32[]{:S(2)}) copy-start(bf16[1,1024,1024]{2,1,0:T(8,128)(2,1)} %param.14) | copy-start | bytes 6291460
  18.3 2.9 %copy-start.2 = (bf16[1,1024,1024]{2,1,0:T(8,128)(2,1)S(1)}, bf16[1,1024,1024]{2,1,0:T(8,128)(2,1)}, u32[]{:S(2)}) copy-start(bf16[1,1024,1024]{2,1,0:T(8,128)(2,1)} %param.15) | copy-start | bytes 6291460
  18.3 3.5 %copy-start.3 = (bf16[1,1024,1024]{2,1,0:T(8,128)(2,1)S(1)}, bf16[1,1024,1024]{2,1,0:T(8,128)(2,1)}, u32[]{:S(2)}) copy-start(bf16[1,1024,1024]{2,1,0:T(8,128)(2,1)} %param.16) | copy-start | bytes 6291460
  18.3 3.5 %copy-start.4 = (f32[1,1024]{1,0:T(1,128)S(1)}, f32[1,1024]{1,0:T(1,128)}, u32[]{:S(2)}) copy-start(f32[1,1024]{1,0:T(1,128)} %refs_2_.3) | copy-start | bytes 12292
  25.3 4.6 %collective-permute-start.3 = (bf16[128,1024]{1,0:T(8,128)(2,1)S(1)}, bf16[128,1024]{1,0:T(8,128)(2,1)S(1)}, u32[]{:S(2)}, u32[]{:S(2)}) collective-permute-start(bf16[128,1024]{1,0:T(8,128)(2,1)S(1)} %get-tuple-element.26), channel_id=1, source_target_pairs={{0,1},{1,0},{2,3},{3,2},{4,5},{5,4},{6,7},{7,6},{8,9},{9,8},{10,11... | collective-permute-start | bytes 786440 | tf_op jit(solution)/shard_map/ppermute | solution.py:331
  27.3 2.6 %collective-permute-start.9 = (bf16[64,1024]{1,0:T(8,128)(2,1)S(1)}, bf16[64,1024]{1,0:T(8,128)(2,1)S(1)}, u32[]{:S(2)}, u32[]{:S(2)}) collective-permute-start(bf16[64,1024]{1,0:T(8,128)(2,1)S(1)} %get-tuple-element.33), channel_id=1, source_target_pairs={{0,1},{1,0},{2,3},{3,2},{4,5},{5,4},{6,7},{7,6},{8,9},{9,8},{10,11... | collective-permute-start | bytes 393224 | tf_op jit(solution)/shard_map/ppermute | solution.py:331
  29.8 1.8 %collective-permute-start.6 = (bf16[64,1024]{1,0:T(8,128)(2,1)S(1)}, bf16[64,1024]{1,0:T(8,128)(2,1)S(1)}, u32[]{:S(2)}, u32[]{:S(2)}) collective-permute-start(bf16[64,1024]{1,0:T(8,128)(2,1)S(1)} %get-tuple-element.29), channel_id=1, source_target_pairs={{0,1},{1,0},{2,3},{3,2},{4,5},{5,4},{6,7},{7,6},{8,9},{9,8},{10,11... | collective-permute-start | bytes 393224 | tf_op jit(solution)/shard_map/ppermute | solution.py:331
  30.0 6.4 %collective-permute-start.11 = (bf16[64,1024]{1,0:T(8,128)(2,1)S(1)}, bf16[64,1024]{1,0:T(8,128)(2,1)S(1)}, u32[]{:S(2)}, u32[]{:S(2)}) collective-permute-start(bf16[64,1024]{1,0:T(8,128)(2,1)S(1)} %get-tuple-element.36), channel_id=1, source_target_pairs={{0,2},{1,3},{2,0},{3,1},{4,6},{5,7},{6,4},{7,5},{8,10},{9,11},{10,... | collective-permute-start | bytes 393224 | tf_op jit(solution)/shard_map/ppermute | solution.py:408
  31.7 7.1 %collective-permute-start.10 = (bf16[64,1024]{1,0:T(8,128)(2,1)S(1)}, bf16[64,1024]{1,0:T(8,128)(2,1)S(1)}, u32[]{:S(2)}, u32[]{:S(2)}) collective-permute-start(bf16[64,1024]{1,0:T(8,128)(2,1)S(1)} %get-tuple-element.35), channel_id=1, source_target_pairs={{0,2},{1,3},{2,0},{3,1},{4,6},{5,7},{6,4},{7,5},{8,10},{9,11},{10,... | collective-permute-start | bytes 393224 | tf_op jit(solution)/shard_map/ppermute | solution.py:408

commit v2 on v1

--- a/solution.py
+++ b/solution.py
@@ -56,16 +56,27 @@
 
 
 def plan(tenants):
-    half = tenants // 2
-    split = half // 2
-    far = [(tenants - 1 - i, tenants - 1 - i - split) for i in range(split)]
-    near = [(half - 1 - i, half - 1 - i - split) for i in range(split - 1)]
-    near.append((split, split))
-    return far, near
-
-
-def pick(core, pair):
-    return pair[0] if pair[0] == pair[1] else jnp.where(core == 0, pair[0], pair[1])
+    half, split = tenants // 2, tenants // 4
+    near = []
+    for i in range(split - 1):
+        near.append(((half - 1 - i, half - 1 - i - split),) * 2)
+    near.append(((split, split),) * 2)
+    far = []
+    for i in range(0, split, 2):
+        top = tenants - 1 - i
+        far.append(((top, top - split), (top - 1, top - 1 - split)))
+    return near, far
+
+
+def halved(pair):
+    return pair[0] == pair[1] != 0
+
+
+def pick(outer, core, table):
+    rows = [
+        row[0] if row[0] == row[1] else jnp.where(core == 0, row[0], row[1]) for row in table
+    ]
+    return jnp.int32(rows[0] if table[0] == table[1] else jnp.where(outer == 0, *rows))
 
 
 def pack_kernel(rounds, cap, runs, tenant_hbm, length_hbm, table_hbm, tokens_hbm, *refs):
@@ -93,14 +104,14 @@
     for copy in tables:
         copy.wait()
     me = lax.axis_index("tenant")
-    core = lax.rem(lax.axis_index("tp"), 2)
+    outer, core = lax.axis_index("tp") // 2, lax.rem(lax.axis_index("tp"), 2)
     side = LANES // cap
     lane = lax.broadcasted_iota(jnp.int32, (1, LANES), 1)
     place = lax.rem(lane, cap)
     part = lane // cap
     rows = lax.broadcasted_iota(jnp.int32, (cap, LANES), 0)
-    for slot, pair in enumerate(rounds):
-        bound = lax.bitwise_xor(me, jnp.int32(pick(core, pair)))
+    for slot, table in enumerate(rounds):
+        bound = lax.bitwise_xor(me, pick(outer, core, table))
         offset = jnp.int32(0)
         seg = jnp.full((1, LANES), -1, jnp.int32)
         for group in range(pairs // side):
@@ -117,7 +128,7 @@
             select[slot * cap : (slot + 1) * cap, group * LANES : (group + 1) * LANES] = (
                 jnp.where(rows == target, 1.0, 0.0).astype(jnp.bfloat16)
             )
-        out_refs[slot][columns // LANES * cap :, :] = jnp.broadcast_to(
+        out_refs[slot][out_refs[slot].shape[0] - SEG_ROWS :, :] = jnp.broadcast_to(
             seg.astype(jnp.float32), (SEG_ROWS, LANES)
         ).astype(jnp.bfloat16)
     heads, band, double = strip_ref.shape
@@ -136,12 +147,19 @@
         packed = jnp.dot(
             select[...], tokens_ref[:, at : at + step], preferred_element_type=jnp.float32
         ).astype(jnp.bfloat16)
-        for slot in range(len(rounds)):
-            for c in range(step // LANES):
-                block = at // LANES + c
-                out_refs[slot][block * cap : (block + 1) * cap, :] = packed[
-                    slot * cap : (slot + 1) * cap, c * LANES : (c + 1) * LANES
-                ]
+        for slot, out_ref in enumerate(out_refs):
+            part = out_ref.shape[0] < columns // LANES * cap
+
+            def store(first, slot=slot, out_ref=out_ref, packed=packed):
+                for c in range(step // LANES):
+                    out_ref[(first + c) * cap : (first + c + 1) * cap, :] = packed[
+                        slot * cap : (slot + 1) * cap, c * LANES : (c + 1) * LANES
+                    ]
+
+            if part:
+                pl.when(core == at // step)(functools.partial(store, 0))
+            else:
+                store(at // LANES)
 
 
 def bias_kernel(strip_ref, bias_ref):
@@ -154,26 +172,55 @@
             bias_ref[head, row : row + band] = turned[:, :extent]
 
 
-def sublayer_kernel(slots, far, half, cap, *refs):
-    count, split = len(slots), half // 2
-    slot_refs = refs[:count]
-    gain_ref, wq_ref, wk_ref, wv_ref, wo_ref, bias_ref, send_ref, keep_ref = refs[
-        count : count + 8
-    ]
-    x, seg, normed, q, k, v, context, score, top, weight = refs[count + 8 :]
+def project_kernel(slots, half, cap, *refs):
+    split = half // 2
+    slot_refs = refs[: len(slots)]
+    gain_ref, wq_ref, wk_ref, wv_ref, x, seg, q, k, v, normed = refs[len(slots) :]
     width = x.shape[1]
+    count = seg.shape[0]
     part = count // 2
     me = lax.axis_index("tenant")
-    t = lax.axis_index("tp")
-    core, outer = lax.rem(t, 2), t // 2
-    for ref, pair in zip(slot_refs, slots):
-        mine = lax.rem(lax.bitwise_xor(me, jnp.int32(pick(core, pair))) // split, 2) == core
+    core = lax.rem(lax.axis_index("tp"), 2)
+
+    def place(ref, at, first):
+        for c in range((ref.shape[0] - SEG_ROWS) // cap):
+            x[
+                pl.ds(pl.multiple_of(at * cap, cap), cap),
+                (first + c) * LANES : (first + c + 1) * LANES,
+            ] = ref[c * cap : (c + 1) * cap, :]
+
+    for ref, (pair, source) in zip(slot_refs, slots):
+        mine = lax.rem(lax.bitwise_xor(me, pick(0, core, (pair, pair))) // split, 2) == core
         at = jnp.where(mine, part, 0) + (pair[0] % part)
-        for c in range(width // LANES):
-            x[pl.ds(pl.multiple_of(at * cap, cap), cap), c * LANES : (c + 1) * LANES] = ref[
-                c * cap : (c + 1) * cap, :
-            ]
-        seg[at] = ref[width // LANES * cap :, :].astype(jnp.float32)
+        if source is None:
+            place(ref, at, 0)
+        else:
+            for side in (0, 1):
+                pl.when(core == (side ^ source))(
+                    functools.partial(place, ref, at, side * (width // LANES // 2))
+                )
+        seg[at] = ref[ref.shape[0] - SEG_ROWS :, :].astype(jnp.float32)
+    total = count * cap
+    step = min(BLOCK, total)
+    for base in range(0, total, step):
+        rows = slice(base, base + step)
+        values = x[rows].astype(jnp.float32)
+        mean_square = jnp.mean(values * values, axis=-1, keepdims=True)
+        normed[...] = (values * lax.rsqrt(mean_square + 1e-06) * gain_ref[...]).astype(
+            jnp.bfloat16
+        )
+        for w_ref, out in ((wq_ref, q), (wk_ref, k), (wv_ref, v)):
+            out[rows] = jnp.dot(
+                normed[...], w_ref[...], preferred_element_type=jnp.float32
+            ).astype(jnp.bfloat16)
+
+
+def attend_kernel(far, half, cap, *refs):
+    x, seg, q, k, v, wo_ref, bias_ref, send_ref, keep_ref, context, score, top, weight = refs
+    count = seg.shape[0]
+    part = count // 2
+    me = lax.axis_index("tenant")
+    outer = lax.axis_index("tp") // 2
     total = count * cap
     step = min(BLOCK, total)
     inner = min(LANES, total)
@@ -188,16 +235,6 @@
     ones = jnp.ones((inner, size), jnp.bfloat16)
     scale = jnp.where(owner, 1.0, 0.0).astype(jnp.float32)
     for base in range(0, total, step):
-        rows = slice(base, base + step)
-        values = x[rows].astype(jnp.float32)
-        mean_square = jnp.mean(values * values, axis=-1, keepdims=True)
-        normed[...] = (values * lax.rsqrt(mean_square + 1e-06) * gain_ref[...]).astype(
-            jnp.bfloat16
-        )
-        for w_ref, out in ((wq_ref, q), (wk_ref, k), (wv_ref, v)):
-            out[...] = jnp.dot(
-                normed[...], w_ref[...], preferred_element_type=jnp.float32
-            ).astype(jnp.bfloat16)
         blocks = step // inner
         for block in range(blocks):
             first = (base + block * inner) // cap
@@ -210,11 +247,12 @@
             allowed = down == jnp.where(code >= 0.0, code, -2.0)
             alive = jnp.broadcast_to(down >= 0.0, (inner, inner))
             at = slice(block * inner, (block + 1) * inner)
+            row = slice(base + at.start, base + at.stop)
             for head in range(heads):
                 cols = slice(head * size, (head + 1) * size)
                 scores = lax.dot_general(
-                    q[at, cols],
-                    k[at, cols],
+                    q[row, cols],
+                    k[row, cols],
                     (((1,), (1,)), ((), ())),
                     preferred_element_type=jnp.float32,
                 )
@@ -229,7 +267,7 @@
                 cols = slice(head * size, (head + 1) * size)
                 both = jnp.dot(
                     weight[head],
-                    jnp.concatenate([v[at, cols], ones], axis=1),
+                    jnp.concatenate([v[row, cols], ones], axis=1),
                     preferred_element_type=jnp.float32,
                 )
                 context[at, cols] = jnp.where(
@@ -248,12 +286,31 @@
                 )
 
 
-def join_kernel(relative, near_keep, near_got, far_keep, far_got, own_ref, send_ref):
+def sublayer_kernel(slots, far, half, cap, *refs):
+    count = len(slots)
+    inputs, (gain_ref, wq_ref, wk_ref, wv_ref, wo_ref, bias_ref, send_ref, keep_ref) = (
+        refs[:count],
+        refs[count : count + 8],
+    )
+    x, seg, normed, q, k, v, context, score, top, weight = refs[count + 8 :]
+    project_kernel(
+        slots, half, cap, *inputs, gain_ref, wq_ref, wk_ref, wv_ref, x, seg, q, k, v, normed
+    )
+    attend_kernel(
+        far, half, cap, x, seg, q, k, v, wo_ref, bias_ref, send_ref, keep_ref, context, score, top, weight
+    )
+
+
+def join_kernel(turn, near_keep, near_got, far_keep, far_got, own_ref, send_ref):
     cap = far_keep.shape[0]
-    rows = slice(relative * cap, (relative + 1) * cap)
+    split = near_keep.shape[0] // cap
+    outer = lax.axis_index("tp") // 2
     half = lax.axis_size("tenant") // 2
-    owner = lax.axis_index("tenant") // half == lax.axis_index("tp") // 2
-    near = near_keep[rows] + near_got[rows].astype(jnp.float32)
+    owner = lax.axis_index("tenant") // half == outer
+    first, later = turn
+    relative = split - 1 - first - lax.rem(outer + later, 2)
+    rows = pl.ds(pl.multiple_of(relative * cap, cap), cap)
+    near = near_keep[rows, :] + near_got[rows, :].astype(jnp.float32)
     far = far_keep[...] + far_got[...].astype(jnp.float32)
     own_ref[...] = jnp.where(owner, near, far)
     send_ref[...] = jnp.where(owner, far, near).astype(jnp.bfloat16)
@@ -263,10 +320,13 @@
     pieces = len(refs) // 2
     own_refs, other_refs, out_ref = refs[:pieces], refs[pieces:-1], refs[-1]
     me = lax.axis_index("tenant")
+    outer = lax.axis_index("tp") // 2
+    direct = pieces // 2
     for i in range(pieces):
-        at = lax.bitwise_xor(lax.rem(me, pieces), pieces - 1 - i)
+        pair = 2 * (i % direct) + lax.rem(outer + i // direct, 2)
+        at = lax.bitwise_xor(lax.rem(me, pieces), pieces - 1 - pair)
         out_ref[pl.ds(pl.multiple_of(at * cap, cap), cap), :] = (
-            own_refs[i][...] + other_refs[i][...].astype(jnp.float32)
+            own_refs[i][...] + other_refs[(i + direct) % pieces][...].astype(jnp.float32)
         ).astype(jnp.bfloat16)
 
 
@@ -285,14 +345,20 @@
 ):
     pairs, cap, width = src_tokens.shape
     half, split = tenants // 2, tenants // 4
-    far, near = plan(tenants)
-    rounds = near + far + [(0, 0)]
-    slot_shape = pltpu.VMEM((width // LANES * cap + SEG_ROWS, LANES), jnp.bfloat16)
+    near, far = plan(tenants)
+    rounds = near + far + [((0, 0),) * 2]
+    slot_shapes = [
+        pltpu.VMEM(
+            (width // LANES * cap // (2 if halved(table[0]) else 1) + SEG_ROWS, LANES),
+            jnp.bfloat16,
+        )
+        for table in rounds
+    ]
     buckets, heads = rel_bias.shape[1:]
     extent = min(LANES, half * cap)
     *packed, strips = pl.pallas_call(
         functools.partial(pack_kernel, rounds, cap, bias_runs(extent, buckets)),
-        out_shape=[slot_shape] * len(rounds)
+        out_shape=slot_shapes
         + [pltpu.VMEM((heads, 8, 2 * extent), jnp.float32)],
         in_specs=[HBM] * 4,
         out_specs=[VMEM] * (len(rounds) + 1),
@@ -320,19 +386,22 @@
         )
     )
 
-    def shift(value, pair):
+    def shift(value, table):
         moves = []
         for u in range(tenants):
             for t in range(tp):
-                moves.append((u * tp + t, (u ^ pair[t % 2]) * tp + t))
+                moves.append((u * tp + t, (u ^ table[t // 2][t % 2]) * tp + t))
         return lax.ppermute(value, ("tenant", "tp"), moves)
 
     def swap(value):
         return lax.ppermute(value, "tp", [(t, t ^ 1) for t in range(tp)])
 
+    def trade(value):
+        return lax.ppermute(value, "tp", [(t, t ^ 2) for t in range(tp)])
+
     arrived = []
-    for value, pair in zip(packed, rounds[:-1]):
-        arrived.append(shift(value, pair))
+    for value, table in zip(packed, rounds[:-1]):
+        arrived.append(shift(value, table))
 
     weights = [w[0] for w in (w_query, w_key, w_value, w_out)]
     bias = pl.pallas_call(
@@ -350,53 +419,57 @@
     def sublayer(rounds_here, values, is_far):
         slots, arrays = [], []
         for pair, value in zip(rounds_here, values):
-            slots.append(pair)
+            slots.append((pair, 0 if halved(pair) else None))
             arrays.append(value)
-            if pair[0] != pair[1]:
-                slots.append(pair[::-1])
+            if pair != (0, 0):
+                slots.append((pair[::-1], 1 if halved(pair) else None))
                 arrays.append(swap(value))
-        count = len(slots)
+        count = 2 * len(rounds_here) if is_far else half
         total = count * cap
         step = min(BLOCK, total)
         inner = min(LANES, total)
         own = w_query.shape[2]
+        params = pltpu.CompilerParams(vmem_limit_bytes=8 * MIB + 10 * total * width)
+        sums = [
+            pltpu.VMEM((total // 2, width), jnp.bfloat16),
+            pltpu.VMEM((total // 2, width), jnp.float32),
+        ]
+        rows = [
+            pltpu.VMEM((total, width), jnp.bfloat16),
+            pltpu.VMEM((count, SEG_ROWS, LANES), jnp.float32),
+        ]
+        projected = [pltpu.VMEM((total, own), jnp.bfloat16)] * 3
+        normed = [pltpu.VMEM((step, width), jnp.bfloat16)]
+        scratch = [
+            pltpu.VMEM((step, own), jnp.bfloat16),
+            pltpu.VMEM((heads, inner, inner), jnp.float32),
+            pltpu.VMEM((heads, inner, inner), jnp.float32),
+            pltpu.VMEM((heads, inner, inner), jnp.bfloat16),
+        ]
+        first = (*map(in_vmem, arrays), norm_gain, *map(in_vmem, weights[:3]))
+        last = (in_vmem(weights[3]), in_vmem(bias))
         send, keep = pl.pallas_call(
             functools.partial(sublayer_kernel, slots, is_far, half, cap),
-            out_shape=[
-                pltpu.VMEM((total // 2, width), jnp.bfloat16),
-                pltpu.VMEM((total // 2, width), jnp.float32),
-            ],
-            in_specs=[VMEM] * (count + 6),
+            out_shape=sums,
+            in_specs=[VMEM] * (len(slots) + 6),
             out_specs=[VMEM] * 2,
-            scratch_shapes=[
-                pltpu.VMEM((total, width), jnp.bfloat16),
-                pltpu.VMEM((count, SEG_ROWS, LANES), jnp.float32),
-                pltpu.VMEM((step, width), jnp.bfloat16),
-                pltpu.VMEM((step, own), jnp.bfloat16),
-                pltpu.VMEM((step, own), jnp.bfloat16),
-                pltpu.VMEM((step, own), jnp.bfloat16),
-                pltpu.VMEM((step, own), jnp.bfloat16),
-                pltpu.VMEM((heads, inner, inner), jnp.float32),
-                pltpu.VMEM((heads, inner, inner), jnp.float32),
-                pltpu.VMEM((heads, inner, inner), jnp.bfloat16),
-            ],
-            compiler_params=pltpu.CompilerParams(
-                vmem_limit_bytes=6 * MIB + 4 * total * width
-            ),
-        )(
-            *map(in_vmem, arrays),
-            norm_gain,
-            *map(in_vmem, weights),
-            in_vmem(bias),
-        )
+            scratch_shapes=rows + normed + projected + scratch,
+            compiler_params=params,
+        )(*first, *last)
         return keep, swap(send)
 
-    near_sums = sublayer(near + [(0, 0)], arrived[: len(near)] + [packed[-1]], False)
+    shifts = [table[0] for table in near] + [(0, 0)]
+    near_sums = sublayer(shifts, arrived[: len(near)] + [packed[-1]], False)
+    direct = arrived[len(near) :]
+    traded = []
+    for value in direct:
+        traded.append(trade(value))
     own, others = [], []
-    for i, pair in enumerate(far):
-        far_sums = sublayer([pair], [arrived[len(near) + i]], True)
+    for i, value in enumerate(direct + traded):
+        later, k = divmod(i, len(direct))
+        far_sums = sublayer([far[k][0]], [value], True)
         kept, send = pl.pallas_call(
-            functools.partial(join_kernel, split - 1 - i),
+            functools.partial(join_kernel, (2 * k, later)),
             out_shape=[
                 pltpu.VMEM((cap, width), jnp.float32),
                 pltpu.VMEM((cap, width), jnp.bfloat16),
@@ -405,7 +478,7 @@
             out_specs=[VMEM] * 2,
             compiler_params=pltpu.CompilerParams(vmem_limit_bytes=MIB),
         )(*map(in_vmem, (*near_sums, *far_sums)))
-        others.append(lax.ppermute(send, "tp", [(t, t ^ 2) for t in range(tp)]))
+        others.append(trade(send))
         own.append(kept)
     return pl.pallas_call(
         functools.partial(finish_kernel, cap),

time: 39.6 us -> 39.8 us (level)
  starting transfers between devices: 12 us -> 14.2 us
  waiting for transfers between devices: 13.6 us -> 12.2 us
  local copies, waits for them, and re-layouts: 3.11 us -> 2.64 us
    ppermute x4 -> x3, waiting for transfers between devices: 7.78 us -> 6.03 us  [shift(): return lax.ppermute(value, ('tenant', 'tp'), moves)]
    ppermute x2 -> x3, starting transfers between devices: 2.83 us -> 3.79 us  [trade(): return lax.ppermute(value, 'tp', [(t, t ^ 2) for t in range(tp)])]
    ppermute x4 -> x3, starting transfers between devices: 7.84 us -> 8.67 us  [shift(): return lax.ppermute(value, ('tenant', 'tp'), moves)]
    ppermute x6 -> x7, starting transfers between devices: 1.31 us -> 1.79 us  [swap(): return lax.ppermute(value, 'tp', [(t, t ^ 1) for t in range(tp)])]
    ppermute x6 -> x7, waiting for transfers between devices: 0.02 us -> 0.5 us  [swap(): return lax.ppermute(value, 'tp', [(t, t ^ 1) for t in range(tp)])]
    unnamed x10, local copies, waits for them, and re-layouts: 3.11 us -> 2.64 us
    ppermute x2 -> x3, waiting for transfers between devices: 5.84 us -> 5.65 us  [trade(): return lax.ppermute(value, 'tp', [(t, t ^ 2) for t in range(tp)])]
  transfers between devices with their start and end apart: 12 -> 13, of which waited for: 5 -> 5; matrix products, arithmetic and copies ran while one was open for 0% -> 0% of each run, Pallas kernels for 20% -> 20%
where the time goes in v2:
time: 39.8 us; the launch traced here: 39.7 us
  starting transfers between devices  14.2 us (36%)
  waiting for transfers between devices  12.2 us (31%)
  Pallas kernels  10.5 us (26%)
  local copies, waits for them, and re-layouts  2.64 us (7%)
    ppermute x3, starting transfers between devices, shift(): return lax.ppermute(value, ('tenant', 'tp'), moves)  8.67 us
    pallas_call x3, Pallas kernels, sublayer(): pl.pallas_call(functools.partial(sublayer_kernel, slots, is_far, half, ca...  7.35 us
    ppermute x3, waiting for transfers between devices, shift(): return lax.ppermute(value, ('tenant', 'tp'), moves)  6.03 us
    ppermute x3, waiting for transfers between devices, trade(): return lax.ppermute(value, 'tp', [(t, t ^ 2) for t in range(tp)])  5.65 us
    ppermute x3, starting transfers between devices, trade(): return lax.ppermute(value, 'tp', [(t, t ^ 2) for t in range(tp)])  3.79 us
    unnamed x10, local copies, waits for them, and re-layouts  2.64 us
    pallas_call x1, Pallas kernels, per_device(): pl.pallas_call(functools.partial(pack_kernel, rounds, cap, bias_runs(exte...  1.95 us
    ppermute x7, starting transfers between devices, swap(): return lax.ppermute(value, 'tp', [(t, t ^ 1) for t in range(tp)])  1.79 us
  transfers between devices with their start and end apart: 13, of which 5 were waited for; matrix products, arithmetic and copies ran while one was open for 0% of the time, Pallas kernels for 20%

profile of v2, /device:TPU:0, one launch (start us, length us, event | category | flops | bytes accessed | tf_op | source)
XLA Modules:
  0.0 39.7 jit_solution(5478553740664798386)
XLA Ops:
  0.0 1.9 %pack.1 = (bf16[520,128]{1,0:T(8,128)(2,1)S(1)}, bf16[264,128]{1,0:T(8,128)(2,1)S(1)}, bf16[520,128]{1,0:T(8,128)(2,1)S(1)}, bf16[520,128]{1,0:T(8,128)(2,1)S(1)}, f32[8,8,256]{2,1,0:T(8,128)S(1)}) custom-call(s32[12]{0:T(128)} %tenant_hbm.1, s32[12]{0:T(128)} %length_hbm.1, f32[8,32]{1,0:T(8,128)} %bitcast.21, bf16[768,1024]{1,0:T(8,128)(2,1)} %bitcast.20), custom_call_target="tpu_custom_call" | custom-call | tf_op jit(solution)/shard_map/pack/pallas_call | solution.py:359
  2.0 6.1 %collective-permute-start.5 = (bf16[520,128]{1,0:T(8,128)(2,1)S(1)}, bf16[520,128]{1,0:T(8,128)(2,1)S(1)}, u32[]{:S(2)}, u32[]{:S(2)}) collective-permute-start(bf16[520,128]{1,0:T(8,128)(2,1)S(1)} %get-tuple-element.26), channel_id=1, source_target_pairs={{0,28},{1,21},{2,26},{3,19},{4,24},{5,17},{6,30},{7,23},{8,20},{9,... | collective-permute-start | bytes 399368 | tf_op jit(solution)/shard_map/ppermute | solution.py:394
  8.0 0.0 collective-permute-start
  8.0 3.8 %collective-permute-done.5.refs_0_ = bf16[520,128]{1,0:T(8,128)(2,1)S(1)} collective-permute-done((bf16[520,128]{1,0:T(8,128)(2,1)S(1)}, bf16[520,128]{1,0:T(8,128)(2,1)S(1)}, u32[]{:S(2)}, u32[]{:S(2)}) %collective-permute-start.5) | collective-permute-done | bytes 133152 | tf_op jit(solution)/shard_map/ppermute | solution.py:394
  11.8 0.5 %collective-permute-start.8 = (bf16[520,128]{1,0:T(8,128)(2,1)S(1)}, bf16[520,128]{1,0:T(8,128)(2,1)S(1)}, u32[]{:S(2)}, u32[]{:S(2)}) collective-permute-start(bf16[520,128]{1,0:T(8,128)(2,1)S(1)} %collective-permute-done.5.refs_0_), channel_id=1, source_target_pairs={{0,2},{1,3},{2,0},{3,1},{4,6},{5,7},{6,4},{7,5},{8,10},{9,11},{10,... | collective-permute-start | bytes 399368 | tf_op jit(solution)/shard_map/ppermute | solution.py:400
  12.3 2.6 %collective-permute-start.2 = (bf16[264,128]{1,0:T(8,128)(2,1)S(1)}, bf16[264,128]{1,0:T(8,128)(2,1)S(1)}, u32[]{:S(2)}, u32[]{:S(2)}) collective-permute-start(bf16[264,128]{1,0:T(8,128)(2,1)S(1)} %get-tuple-element.21), channel_id=1, source_target_pairs={{0,8},{1,9},{2,10},{3,11},{4,12},{5,13},{6,14},{7,15},{8,0},{9,1},... | collective-permute-start | bytes 202760 | tf_op jit(solution)/shard_map/ppermute | solution.py:394
  14.9 2.3 %collective-permute-done.2.refs_2_ = bf16[264,128]{1,0:T(8,128)(2,1)S(1)} collective-permute-done((bf16[264,128]{1,0:T(8,128)(2,1)S(1)}, bf16[264,128]{1,0:T(8,128)(2,1)S(1)}, u32[]{:S(2)}, u32[]{:S(2)}) %collective-permute-start.2) | collective-permute-done | bytes 67616 | tf_op jit(solution)/shard_map/ppermute | solution.py:394
  17.2 0.0 collective-permute-start.3
  17.2 0.5 %collective-permute-start.6 = (bf16[520,128]{1,0:T(8,128)(2,1)S(1)}, bf16[520,128]{1,0:T(8,128)(2,1)S(1)}, u32[]{:S(2)}, u32[]{:S(2)}) collective-permute-start(bf16[520,128]{1,0:T(8,128)(2,1)S(1)} %collective-permute-done.5.refs_0_), channel_id=1, source_target_pairs={{0,1},{1,0},{2,3},{3,2},{4,5},{5,4},{6,7},{7,6},{8,9},{9,8},{10,11... | collective-permute-start | bytes 399368 | tf_op jit(solution)/shard_map/ppermute | solution.py:397
  17.7 0.0 collective-permute-done.refs_0_
  17.7 0.0 collective-permute-start.1
  17.7 0.0 collective-permute-done.8.refs_0_
  17.7 0.5 %collective-permute-start.9 = (bf16[520,128]{1,0:T(8,128)(2,1)S(1)}, bf16[520,128]{1,0:T(8,128)(2,1)S(1)}, u32[]{:S(2)}, u32[]{:S(2)}) collective-permute-start(bf16[520,128]{1,0:T(8,128)(2,1)S(1)} %collective-permute-done.8.refs_0_), channel_id=1, source_target_pairs={{0,1},{1,0},{2,3},{3,2},{4,5},{5,4},{6,7},{7,6},{8,9},{9,8},{10,11... | collective-permute-start | bytes 399368 | tf_op jit(solution)/shard_map/ppermute | solution.py:397
  18.2 0.0 copy-start
  18.2 0.0 copy-start.1
  18.2 0.0 copy-start.2
  18.2 0.0 copy-start.3
  18.2 0.0 copy-start.4
  18.2 0.3 prepare.1.refs_10_.refs_7_
  18.5 0.0 collective-permute-done.3.refs_3_
  18.6 0.5 %collective-permute-done.1.refs_1_ = bf16[520,128]{1,0:T(8,128)(2,1)S(1)} collective-permute-done((bf16[520,128]{1,0:T(8,128)(2,1)S(1)}, bf16[520,128]{1,0:T(8,128)(2,1)S(1)}, u32[]{:S(2)}, u32[]{:S(2)}) %collective-permute-start.1) | collective-permute-done | bytes 133152 | tf_op jit(solution)/shard_map/ppermute | solution.py:397
  19.0 0.8 %copy-done = bf16[1,1024,1024]{2,1,0:T(8,128)(2,1)S(1)} copy-done((bf16[1,1024,1024]{2,1,0:T(8,128)(2,1)S(1)}, bf16[1,1024,1024]{2,1,0:T(8,128)(2,1)}, u32[]{:S(2)}) %copy-start) | copy-done | bytes 2097176
  19.8 0.6 %copy-done.1 = bf16[1,1024,1024]{2,1,0:T(8,128)(2,1)S(1)} copy-done((bf16[1,1024,1024]{2,1,0:T(8,128)(2,1)S(1)}, bf16[1,1024,1024]{2,1,0:T(8,128)(2,1)}, u32[]{:S(2)}) %copy-start.1) | copy-done | bytes 2097176
  20.4 0.6 %copy-done.2 = bf16[1,1024,1024]{2,1,0:T(8,128)(2,1)S(1)} copy-done((bf16[1,1024,1024]{2,1,0:T(8,128)(2,1)S(1)}, bf16[1,1024,1024]{2,1,0:T(8,128)(2,1)}, u32[]{:S(2)}) %copy-start.2) | copy-done | bytes 2097176
  21.1 0.6 %copy-done.3 = bf16[1,1024,1024]{2,1,0:T(8,128)(2,1)S(1)} copy-done((bf16[1,1024,1024]{2,1,0:T(8,128)(2,1)S(1)}, bf16[1,1024,1024]{2,1,0:T(8,128)(2,1)}, u32[]{:S(2)}) %copy-start.3) | copy-done | bytes 2097176
  21.7 0.0 copy-done.4
  21.7 3.5 %shard_map.91 = (bf16[128,1024]{1,0:T(8,128)(2,1)S(1)}, f32[128,1024]{1,0:T(8,128)S(1)}) custom-call(bf16[520,128]{1,0:T(8,128)(2,1)S(1)} %collective-permute-done.refs_0_, bf16[520,128]{1,0:T(8,128)(2,1)S(1)} %collective-permute-done.1.refs_1_, bf16[264,128]{1,0:T(8,128)(2,1)S(1)} %collective-permute-done.2.refs_2_, ...), custom_call_target="tpu_custom_call" | custom-call | tf_op jit(solution)/shard_map/pallas_call | solution.py:451
  25.2 0.1 collective-permute-start.4
  25.3 0.0 collective-permute-done.6.refs_1_
  25.3 1.9 %shard_map.92 = (bf16[64,1024]{1,0:T(8,128)(2,1)S(1)}, f32[64,1024]{1,0:T(8,128)S(1)}) custom-call(bf16[520,128]{1,0:T(8,128)(2,1)S(1)} %collective-permute-done.5.refs_0_, bf16[520,128]{1,0:T(8,128)(2,1)S(1)} %collective-permute-done.6.refs_1_, f32[1,1024]{1,0:T(1,128)S(1)} %copy-done.4, bf16[1024,1024]{1,0:T(8,128)(2,1)S(1)} %bitcast.9, ...), custom_call_target="tpu_custom_call" | custom-call | tf_op jit(solution)/shard_map/pallas_call | solution.py:451
  27.3 0.5 %collective-permute-start.7 = (bf16[64,1024]{1,0:T(8,128)(2,1)S(1)}, bf16[64,1024]{1,0:T(8,128)(2,1)S(1)}, u32[]{:S(2)}, u32[]{:S(2)}) collective-permute-start(bf16[64,1024]{1,0:T(8,128)(2,1)S(1)} %get-tuple-element.28), channel_id=1, source_target_pairs={{0,1},{1,0},{2,3},{3,2},{4,5},{5,4},{6,7},{7,6},{8,9},{9,8},{10,11... | collective-permute-start | bytes 393224 | tf_op jit(solution)/shard_map/ppermute | solution.py:397
  27.8 0.0 collective-permute-done.9.refs_1_
  27.8 1.9 %shard_map.94 = (bf16[64,1024]{1,0:T(8,128)(2,1)S(1)}, f32[64,1024]{1,0:T(8,128)S(1)}) custom-call(bf16[520,128]{1,0:T(8,128)(2,1)S(1)} %collective-permute-done.8.refs_0_, bf16[520,128]{1,0:T(8,128)(2,1)S(1)} %collective-permute-done.9.refs_1_, f32[1,1024]{1,0:T(1,128)S(1)} %copy-done.4, bf16[1024,1024]{1,0:T(8,128)(2,1)S(1)} %bitcast.10, ...), custom_call_target="tpu_custom_call" | custom-call | tf_op jit(solution)/shard_map/pallas_call | solution.py:451
  29.7 0.1 collective-permute-start.10
  29.8 0.0 collective-permute-done.7.far_got
  29.8 0.0 collective-permute-done.4.near_got
  29.8 0.1 shard_map.93
  29.9 2.1 %collective-permute-start.11 = (bf16[64,1024]{1,0:T(8,128)(2,1)S(1)}, bf16[64,1024]{1,0:T(8,128)(2,1)S(1)}, u32[]{:S(2)}, u32[]{:S(2)}) collective-permute-start(bf16[64,1024]{1,0:T(8,128)(2,1)S(1)} %get-tuple-element.33), channel_id=1, source_target_pairs={{0,2},{1,3},{2,0},{3,1},{4,6},{5,7},{6,4},{7,5},{8,10},{9,11},{10,... | collective-permute-start | bytes 393224 | tf_op jit(solution)/shard_map/ppermute | solution.py:400
  32.0 0.0 collective-permute-done.10.far_got
  32.0 0.1 shard_map.95
  32.1 1.2 %collective-permute-start.12 = (bf16[64,1024]{1,0:T(8,128)(2,1)S(1)}, bf16[64,1024]{1,0:T(8,128)(2,1)S(1)}, u32[]{:S(2)}, u32[]{:S(2)}) collective-permute-start(bf16[64,1024]{1,0:T(8,128)(2,1)S(1)} %get-tuple-element.34), channel_id=1, source_target_pairs={{0,2},{1,3},{2,0},{3,1},{4,6},{5,7},{6,4},{7,5},{8,10},{9,11},{10,... | collective-permute-start | bytes 393224 | tf_op jit(solution)/shard_map/ppermute | solution.py:400
  33.3 3.1 %collective-permute-done.11.refs_2_ = bf16[64,1024]{1,0:T(8,128)(2,1)S(1)} collective-permute-done((bf16[64,1024]{1,0:T(8,128)(2,1)S(1)}, bf16[64,1024]{1,0:T(8,128)(2,1)S(1)}, u32[]{:S(2)}, u32[]{:S(2)}) %collective-permute-start.11) | collective-permute-done | bytes 131104 | tf_op jit(solution)/shard_map/ppermute | solution.py:400
  36.4 2.6 %collective-permute-done.12.refs_3_ = bf16[64,1024]{1,0:T(8,128)(2,1)S(1)} collective-permute-done((bf16[64,1024]{1,0:T(8,128)(2,1)S(1)}, bf16[64,1024]{1,0:T(8,128)(2,1)S(1)}, u32[]{:S(2)}, u32[]{:S(2)}) %collective-permute-start.12) | collective-permute-done | bytes 131104 | tf_op jit(solution)/shard_map/ppermute | solution.py:400
  38.9 0.8 %finish.1 = bf16[128,1024]{1,0:T(8,128)(2,1)} custom-call(f32[64,1024]{1,0:T(8,128)S(1)} %get-tuple-element.29.refs_0_, f32[64,1024]{1,0:T(8,128)S(1)} %get-tuple-element.32.refs_1_, bf16[64,1024]{1,0:T(8,128)(2,1)S(1)} %collective-permute-done.11.refs_2_, bf16[64,1024]{1,0:T(8,128)(2,1)S(1)} %collective-permute-done.12.refs_3_), custom_call_target="tpu_custom_call" | custom-call | tf_op jit(solution)/shard_map/finish/pallas_call | solution.py:483
Async XLA Ops:
  2.0 9.8 %collective-permute-start.5 = (bf16[520,128]{1,0:T(8,128)(2,1)S(1)}, bf16[520,128]{1,0:T(8,128)(2,1)S(1)}, u32[]{:S(2)}, u32[]{:S(2)}) collective-permute-start(bf16[520,128]{1,0:T(8,128)(2,1)S(1)} %get-tuple-element.26), channel_id=1, source_target_pairs={{0,28},{1,21},{2,26},{3,19},{4,24},{5,17},{6,30},{7,23},{8,20},{9,... | collective-permute-start | bytes 399368 | tf_op jit(solution)/shard_map/ppermute | solution.py:394
  8.0 9.7 %collective-permute-start = (bf16[520,128]{1,0:T(8,128)(2,1)S(1)}, bf16[520,128]{1,0:T(8,128)(2,1)S(1)}, u32[]{:S(2)}, u32[]{:S(2)}) collective-permute-start(bf16[520,128]{1,0:T(8,128)(2,1)S(1)} %get-tuple-element.20), channel_id=1, source_target_pairs={{0,12},{1,5},{2,14},{3,7},{4,8},{5,1},{6,10},{7,3},{8,4},{9,13},{1... | collective-permute-start | bytes 399368 | tf_op jit(solution)/shard_map/ppermute | solution.py:394
  11.8 5.9 %collective-permute-start.8 = (bf16[520,128]{1,0:T(8,128)(2,1)S(1)}, bf16[520,128]{1,0:T(8,128)(2,1)S(1)}, u32[]{:S(2)}, u32[]{:S(2)}) collective-permute-start(bf16[520,128]{1,0:T(8,128)(2,1)S(1)} %collective-permute-done.5.refs_0_), channel_id=1, source_target_pairs={{0,2},{1,3},{2,0},{3,1},{4,6},{5,7},{6,4},{7,5},{8,10},{9,11},{10,... | collective-permute-start | bytes 399368 | tf_op jit(solution)/shard_map/ppermute | solution.py:400
  12.3 4.9 %collective-permute-start.2 = (bf16[264,128]{1,0:T(8,128)(2,1)S(1)}, bf16[264,128]{1,0:T(8,128)(2,1)S(1)}, u32[]{:S(2)}, u32[]{:S(2)}) collective-permute-start(bf16[264,128]{1,0:T(8,128)(2,1)S(1)} %get-tuple-element.21), channel_id=1, source_target_pairs={{0,8},{1,9},{2,10},{3,11},{4,12},{5,13},{6,14},{7,15},{8,0},{9,1},... | collective-permute-start | bytes 202760 | tf_op jit(solution)/shard_map/ppermute | solution.py:394
  17.2 1.4 %collective-permute-start.3 = (bf16[264,128]{1,0:T(8,128)(2,1)S(1)}, bf16[264,128]{1,0:T(8,128)(2,1)S(1)}, u32[]{:S(2)}, u32[]{:S(2)}) collective-permute-start(bf16[264,128]{1,0:T(8,128)(2,1)S(1)} %collective-permute-done.2.refs_2_), channel_id=1, source_target_pairs={{0,1},{1,0},{2,3},{3,2},{4,5},{5,4},{6,7},{7,6},{8,9},{9,8},{10,11... | collective-permute-start | bytes 202760 | tf_op jit(solution)/shard_map/ppermute | solution.py:397
  17.2 8.2 %collective-permute-start.6 = (bf16[520,128]{1,0:T(8,128)(2,1)S(1)}, bf16[520,128]{1,0:T(8,128)(2,1)S(1)}, u32[]{:S(2)}, u32[]{:S(2)}) collective-permute-start(bf16[520,128]{1,0:T(8,128)(2,1)S(1)} %collective-permute-done.5.refs_0_), channel_id=1, source_target_pairs={{0,1},{1,0},{2,3},{3,2},{4,5},{5,4},{6,7},{7,6},{8,9},{9,8},{10,11... | collective-permute-start | bytes 399368 | tf_op jit(solution)/shard_map/ppermute | solution.py:397
  17.7 1.4 %collective-permute-start.1 = (bf16[520,128]{1,0:T(8,128)(2,1)S(1)}, bf16[520,128]{1,0:T(8,128)(2,1)S(1)}, u32[]{:S(2)}, u32[]{:S(2)}) collective-permute-start(bf16[520,128]{1,0:T(8,128)(2,1)S(1)} %collective-permute-done.refs_0_), channel_id=1, source_target_pairs={{0,1},{1,0},{2,3},{3,2},{4,5},{5,4},{6,7},{7,6},{8,9},{9,8},{10,11... | collective-permute-start | bytes 399368 | tf_op jit(solution)/shard_map/ppermute | solution.py:397
  17.7 10.1 %collective-permute-start.9 = (bf16[520,128]{1,0:T(8,128)(2,1)S(1)}, bf16[520,128]{1,0:T(8,128)(2,1)S(1)}, u32[]{:S(2)}, u32[]{:S(2)}) collective-permute-start(bf16[520,128]{1,0:T(8,128)(2,1)S(1)} %collective-permute-done.8.refs_0_), channel_id=1, source_target_pairs={{0,1},{1,0},{2,3},{3,2},{4,5},{5,4},{6,7},{7,6},{8,9},{9,8},{10,11... | collective-permute-start | bytes 399368 | tf_op jit(solution)/shard_map/ppermute | solution.py:397
  18.2 1.6 %copy-start = (bf16[1,1024,1024]{2,1,0:T(8,128)(2,1)S(1)}, bf16[1,1024,1024]{2,1,0:T(8,128)(2,1)}, u32[]{:S(2)}) copy-start(bf16[1,1024,1024]{2,1,0:T(8,128)(2,1)} %param.13) | copy-start | bytes 6291460
  18.2 2.2 %copy-start.1 = (bf16[1,1024,1024]{2,1,0:T(8,128)(2,1)S(1)}, bf16[1,1024,1024]{2,1,0:T(8,128)(2,1)}, u32[]{:S(2)}) copy-start(bf16[1,1024,1024]{2,1,0:T(8,128)(2,1)} %param.14) | copy-start | bytes 6291460
  18.2 2.9 %copy-start.2 = (bf16[1,1024,1024]{2,1,0:T(8,128)(2,1)S(1)}, bf16[1,1024,1024]{2,1,0:T(8,128)(2,1)}, u32[]{:S(2)}) copy-start(bf16[1,1024,1024]{2,1,0:T(8,128)(2,1)} %param.15) | copy-start | bytes 6291460
  18.2 3.5 %copy-start.3 = (bf16[1,1024,1024]{2,1,0:T(8,128)(2,1)S(1)}, bf16[1,1024,1024]{2,1,0:T(8,128)(2,1)}, u32[]{:S(2)}) copy-start(bf16[1,1024,1024]{2,1,0:T(8,128)(2,1)} %param.16) | copy-start | bytes 6291460
  18.2 3.5 %copy-start.4 = (f32[1,1024]{1,0:T(1,128)S(1)}, f32[1,1024]{1,0:T(1,128)}, u32[]{:S(2)}) copy-start(f32[1,1024]{1,0:T(1,128)} %refs_2_.3) | copy-start | bytes 12292
  25.2 4.7 %collective-permute-start.4 = (bf16[128,1024]{1,0:T(8,128)(2,1)S(1)}, bf16[128,1024]{1,0:T(8,128)(2,1)S(1)}, u32[]{:S(2)}, u32[]{:S(2)}) collective-permute-start(bf16[128,1024]{1,0:T(8,128)(2,1)S(1)} %get-tuple-element.25), channel_id=1, source_target_pairs={{0,1},{1,0},{2,3},{3,2},{4,5},{5,4},{6,7},{7,6},{8,9},{9,8},{10,11... | collective-permute-start | bytes 786440 | tf_op jit(solution)/shard_map/ppermute | solution.py:397
  27.3 2.6 %collective-permute-start.7 = (bf16[64,1024]{1,0:T(8,128)(2,1)S(1)}, bf16[64,1024]{1,0:T(8,128)(2,1)S(1)}, u32[]{:S(2)}, u32[]{:S(2)}) collective-permute-start(bf16[64,1024]{1,0:T(8,128)(2,1)S(1)} %get-tuple-element.28), channel_id=1, source_target_pairs={{0,1},{1,0},{2,3},{3,2},{4,5},{5,4},{6,7},{7,6},{8,9},{9,8},{10,11... | collective-permute-start | bytes 393224 | tf_op jit(solution)/shard_map/ppermute | solution.py:397
  29.7 2.3 %collective-permute-start.10 = (bf16[64,1024]{1,0:T(8,128)(2,1)S(1)}, bf16[64,1024]{1,0:T(8,128)(2,1)S(1)}, u32[]{:S(2)}, u32[]{:S(2)}) collective-permute-start(bf16[64,1024]{1,0:T(8,128)(2,1)S(1)} %get-tuple-element.31), channel_id=1, source_target_pairs={{0,1},{1,0},{2,3},{3,2},{4,5},{5,4},{6,7},{7,6},{8,9},{9,8},{10,11... | collective-permute-start | bytes 393224 | tf_op jit(solution)/shard_map/ppermute | solution.py:397
  29.9 6.4 %collective-permute-start.11 = (bf16[64,1024]{1,0:T(8,128)(2,1)S(1)}, bf16[64,1024]{1,0:T(8,128)(2,1)S(1)}, u32[]{:S(2)}, u32[]{:S(2)}) collective-permute-start(bf16[64,1024]{1,0:T(8,128)(2,1)S(1)} %get-tuple-element.33), channel_id=1, source_target_pairs={{0,2},{1,3},{2,0},{3,1},{4,6},{5,7},{6,4},{7,5},{8,10},{9,11},{10,... | collective-permute-start | bytes 393224 | tf_op jit(solution)/shard_map/ppermute | solution.py:400
  32.1 6.8 %collective-permute-start.12 = (bf16[64,1024]{1,0:T(8,128)(2,1)S(1)}, bf16[64,1024]{1,0:T(8,128)(2,1)S(1)}, u32[]{:S(2)}, u32[]{:S(2)}) collective-permute-start(bf16[64,1024]{1,0:T(8,128)(2,1)S(1)} %get-tuple-element.34), channel_id=1, source_target_pairs={{0,2},{1,3},{2,0},{3,1},{4,6},{5,7},{6,4},{7,5},{8,10},{9,11},{10,... | collective-permute-start | bytes 393224 | tf_op jit(solution)/shard_map/ppermute | solution.py:400

commit v3 on v2

--- a/solution.py
+++ b/solution.py
@@ -416,7 +416,7 @@
         name="prepare",
     )(in_vmem(strips))
 
-    def sublayer(rounds_here, values, is_far):
+    def sublayer(rounds_here, values, is_far, parts):
         slots, arrays = [], []
         for pair, value in zip(rounds_here, values):
             slots.append((pair, 0 if halved(pair) else None))
@@ -429,7 +429,8 @@
         step = min(BLOCK, total)
         inner = min(LANES, total)
         own = w_query.shape[2]
-        params = pltpu.CompilerParams(vmem_limit_bytes=8 * MIB + 10 * total * width)
+        params = pltpu.CompilerParams(
+            vmem_limit_bytes=8 * MIB + 10 * total * width)
         sums = [
             pltpu.VMEM((total // 2, width), jnp.bfloat16),
             pltpu.VMEM((total // 2, width), jnp.float32),
@@ -448,18 +449,36 @@
         ]
         first = (*map(in_vmem, arrays), norm_gain, *map(in_vmem, weights[:3]))
         last = (in_vmem(weights[3]), in_vmem(bias))
-        send, keep = pl.pallas_call(
-            functools.partial(sublayer_kernel, slots, is_far, half, cap),
-            out_shape=sums,
-            in_specs=[VMEM] * (len(slots) + 6),
-            out_specs=[VMEM] * 2,
-            scratch_shapes=rows + normed + projected + scratch,
-            compiler_params=params,
-        )(*first, *last)
+        if parts == 1:
+            send, keep = pl.pallas_call(
+                functools.partial(sublayer_kernel, slots, is_far, half, cap),
+                out_shape=sums,
+                in_specs=[VMEM] * (len(slots) + 6),
+                out_specs=[VMEM] * 2,
+                scratch_shapes=rows + normed + projected + scratch,
+                compiler_params=params,
+            )(*first, *last)
+        else:
+            made = pl.pallas_call(
+                functools.partial(project_kernel, slots, half, cap),
+                out_shape=rows + projected,
+                in_specs=[VMEM] * (len(slots) + 4),
+                out_specs=[VMEM] * 5,
+                scratch_shapes=normed,
+                compiler_params=params,
+            )(*first)
+            send, keep = pl.pallas_call(
+                functools.partial(attend_kernel, is_far, half, cap),
+                out_shape=sums,
+                in_specs=[VMEM] * 7,
+                out_specs=[VMEM] * 2,
+                scratch_shapes=scratch,
+                compiler_params=params,
+            )(*map(in_vmem, made), *last)
         return keep, swap(send)
 
     shifts = [table[0] for table in near] + [(0, 0)]
-    near_sums = sublayer(shifts, arrived[: len(near)] + [packed[-1]], False)
+    near_sums = sublayer(shifts, arrived[: len(near)] + [packed[-1]], False, 2)
     direct = arrived[len(near) :]
     traded = []
     for value in direct:
@@ -467,7 +486,7 @@
     own, others = [], []
     for i, value in enumerate(direct + traded):
         later, k = divmod(i, len(direct))
-        far_sums = sublayer([far[k][0]], [value], True)
+        far_sums = sublayer([far[k][0]], [value], True, 1)
         kept, send = pl.pallas_call(
             functools.partial(join_kernel, (2 * k, later)),
             out_shape=[

time: 39.8 us -> 39.4 us (0.990)
  local copies, waits for them, and re-layouts: 2.64 us -> 2.03 us
    pallas_call x0 -> x2, Pallas kernels: none -> 3.67 us  [the longest x1 2.05 us: sublayer(): pl.pallas_call(functools.partial(project_kernel, slots, half, cap), out_s...]
    pallas_call x3 -> x2, Pallas kernels: 7.35 us -> 3.84 us  [sublayer(): pl.pallas_call(functools.partial(sublayer_kernel, slots, is_far, half, ca...]
    unnamed x10, local copies, waits for them, and re-layouts: 2.64 us -> 2.03 us
where the time goes in v3:
time: 39.4 us; the launch traced here: 39.2 us
  starting transfers between devices  14.2 us (36%)
  waiting for transfers between devices  12.2 us (31%)
  Pallas kernels  10.7 us (27%)
  local copies, waits for them, and re-layouts  2.03 us (5%)
    ppermute x3, starting transfers between devices, shift(): return lax.ppermute(value, ('tenant', 'tp'), moves)  8.67 us
    ppermute x3, waiting for transfers between devices, shift(): return lax.ppermute(value, ('tenant', 'tp'), moves)  6.03 us
    ppermute x3, waiting for transfers between devices, trade(): return lax.ppermute(value, 'tp', [(t, t ^ 2) for t in range(tp)])  5.64 us
    pallas_call x2, Pallas kernels, sublayer(): pl.pallas_call(functools.partial(sublayer_kernel, slots, is_far, half, ca...  3.84 us
    ppermute x3, starting transfers between devices, trade(): return lax.ppermute(value, 'tp', [(t, t ^ 2) for t in range(tp)])  3.79 us
    pallas_call x1, Pallas kernels, sublayer(): pl.pallas_call(functools.partial(project_kernel, slots, half, cap), out_s...  2.05 us
    unnamed x10, local copies, waits for them, and re-layouts  2.03 us
    pallas_call x1, Pallas kernels, per_device(): pl.pallas_call(functools.partial(pack_kernel, rounds, cap, bias_runs(exte...  1.95 us
  transfers between devices with their start and end apart: 13, of which 5 were waited for; matrix products, arithmetic and copies ran while one was open for 0% of the time, Pallas kernels for 20%

profile of v3, /device:TPU:0, one launch (start us, length us, event | category | flops | bytes accessed | tf_op | source)
XLA Modules:
  0.0 39.2 jit_solution(3287992149673791152)
XLA Ops:
  0.0 1.9 %pack.1 = (bf16[520,128]{1,0:T(8,128)(2,1)S(1)}, bf16[264,128]{1,0:T(8,128)(2,1)S(1)}, bf16[520,128]{1,0:T(8,128)(2,1)S(1)}, bf16[520,128]{1,0:T(8,128)(2,1)S(1)}, f32[8,8,256]{2,1,0:T(8,128)S(1)}) custom-call(s32[12]{0:T(128)} %tenant_hbm.1, s32[12]{0:T(128)} %length_hbm.1, f32[8,32]{1,0:T(8,128)} %bitcast.21, bf16[768,1024]{1,0:T(8,128)(2,1)} %bitcast.20), custom_call_target="tpu_custom_call" | custom-call | tf_op jit(solution)/shard_map/pack/pallas_call | solution.py:359
  2.0 6.1 %collective-permute-start.5 = (bf16[520,128]{1,0:T(8,128)(2,1)S(1)}, bf16[520,128]{1,0:T(8,128)(2,1)S(1)}, u32[]{:S(2)}, u32[]{:S(2)}) collective-permute-start(bf16[520,128]{1,0:T(8,128)(2,1)S(1)} %get-tuple-element.36), channel_id=1, source_target_pairs={{0,28},{1,21},{2,26},{3,19},{4,24},{5,17},{6,30},{7,23},{8,20},{9,... | collective-permute-start | bytes 399368 | tf_op jit(solution)/shard_map/ppermute | solution.py:394
  8.0 0.0 collective-permute-start
  8.0 3.8 %collective-permute-done.5.refs_0_ = bf16[520,128]{1,0:T(8,128)(2,1)S(1)} collective-permute-done((bf16[520,128]{1,0:T(8,128)(2,1)S(1)}, bf16[520,128]{1,0:T(8,128)(2,1)S(1)}, u32[]{:S(2)}, u32[]{:S(2)}) %collective-permute-start.5) | collective-permute-done | bytes 133152 | tf_op jit(solution)/shard_map/ppermute | solution.py:394
  11.8 0.5 %collective-permute-start.8 = (bf16[520,128]{1,0:T(8,128)(2,1)S(1)}, bf16[520,128]{1,0:T(8,128)(2,1)S(1)}, u32[]{:S(2)}, u32[]{:S(2)}) collective-permute-start(bf16[520,128]{1,0:T(8,128)(2,1)S(1)} %collective-permute-done.5.refs_0_), channel_id=1, source_target_pairs={{0,2},{1,3},{2,0},{3,1},{4,6},{5,7},{6,4},{7,5},{8,10},{9,11},{10,... | collective-permute-start | bytes 399368 | tf_op jit(solution)/shard_map/ppermute | solution.py:400
  12.3 2.6 %collective-permute-start.2 = (bf16[264,128]{1,0:T(8,128)(2,1)S(1)}, bf16[264,128]{1,0:T(8,128)(2,1)S(1)}, u32[]{:S(2)}, u32[]{:S(2)}) collective-permute-start(bf16[264,128]{1,0:T(8,128)(2,1)S(1)} %get-tuple-element.26), channel_id=1, source_target_pairs={{0,8},{1,9},{2,10},{3,11},{4,12},{5,13},{6,14},{7,15},{8,0},{9,1},... | collective-permute-start | bytes 202760 | tf_op jit(solution)/shard_map/ppermute | solution.py:394
  14.9 2.3 %collective-permute-done.2.refs_2_ = bf16[264,128]{1,0:T(8,128)(2,1)S(1)} collective-permute-done((bf16[264,128]{1,0:T(8,128)(2,1)S(1)}, bf16[264,128]{1,0:T(8,128)(2,1)S(1)}, u32[]{:S(2)}, u32[]{:S(2)}) %collective-permute-start.2) | collective-permute-done | bytes 67616 | tf_op jit(solution)/shard_map/ppermute | solution.py:394
  17.2 0.0 collective-permute-start.3
  17.2 0.5 %collective-permute-start.6 = (bf16[520,128]{1,0:T(8,128)(2,1)S(1)}, bf16[520,128]{1,0:T(8,128)(2,1)S(1)}, u32[]{:S(2)}, u32[]{:S(2)}) collective-permute-start(bf16[520,128]{1,0:T(8,128)(2,1)S(1)} %collective-permute-done.5.refs_0_), channel_id=1, source_target_pairs={{0,1},{1,0},{2,3},{3,2},{4,5},{5,4},{6,7},{7,6},{8,9},{9,8},{10,11... | collective-permute-start | bytes 399368 | tf_op jit(solution)/shard_map/ppermute | solution.py:397
  17.7 0.0 collective-permute-done.refs_0_
  17.7 0.0 collective-permute-start.1
  17.7 0.0 collective-permute-done.8.refs_0_
  17.7 0.5 %collective-permute-start.9 = (bf16[520,128]{1,0:T(8,128)(2,1)S(1)}, bf16[520,128]{1,0:T(8,128)(2,1)S(1)}, u32[]{:S(2)}, u32[]{:S(2)}) collective-permute-start(bf16[520,128]{1,0:T(8,128)(2,1)S(1)} %collective-permute-done.8.refs_0_), channel_id=1, source_target_pairs={{0,1},{1,0},{2,3},{3,2},{4,5},{5,4},{6,7},{7,6},{8,9},{9,8},{10,11... | collective-permute-start | bytes 399368 | tf_op jit(solution)/shard_map/ppermute | solution.py:397
  18.2 0.0 copy-start.1
  18.2 0.0 copy-start.2
  18.2 0.0 copy-start.3
  18.2 0.0 copy-start.4
  18.2 0.3 prepare.1.refs_6_.refs_7_
  18.5 0.0 collective-permute-done.3.refs_3_
  18.5 0.5 %collective-permute-done.1.refs_1_ = bf16[520,128]{1,0:T(8,128)(2,1)S(1)} collective-permute-done((bf16[520,128]{1,0:T(8,128)(2,1)S(1)}, bf16[520,128]{1,0:T(8,128)(2,1)S(1)}, u32[]{:S(2)}, u32[]{:S(2)}) %collective-permute-start.1) | collective-permute-done | bytes 133152 | tf_op jit(solution)/shard_map/ppermute | solution.py:397
  19.0 0.8 %copy-done.1 = bf16[1,1024,1024]{2,1,0:T(8,128)(2,1)S(1)} copy-done((bf16[1,1024,1024]{2,1,0:T(8,128)(2,1)S(1)}, bf16[1,1024,1024]{2,1,0:T(8,128)(2,1)}, u32[]{:S(2)}) %copy-start.1) | copy-done | bytes 2097176
  19.8 0.6 %copy-done.2 = bf16[1,1024,1024]{2,1,0:T(8,128)(2,1)S(1)} copy-done((bf16[1,1024,1024]{2,1,0:T(8,128)(2,1)S(1)}, bf16[1,1024,1024]{2,1,0:T(8,128)(2,1)}, u32[]{:S(2)}) %copy-start.2) | copy-done | bytes 2097176
  20.4 0.6 %copy-done.3 = bf16[1,1024,1024]{2,1,0:T(8,128)(2,1)S(1)} copy-done((bf16[1,1024,1024]{2,1,0:T(8,128)(2,1)S(1)}, bf16[1,1024,1024]{2,1,0:T(8,128)(2,1)}, u32[]{:S(2)}) %copy-start.3) | copy-done | bytes 2097176
  21.1 0.0 copy-done.4
  21.1 0.0 copy-start
  21.1 2.1 %shard_map.91 = (bf16[256,1024]{1,0:T(8,128)(2,1)S(1)}, f32[4,8,128]{2,1,0:T(8,128)S(1)}, bf16[256,1024]{1,0:T(8,128)(2,1)S(1)}, bf16[256,1024]{1,0:T(8,128)(2,1)S(1)}, bf16[256,1024]{1,0:T(8,128)(2,1)S(1)}) custom-call(bf16[520,128]{1,0:T(8,128)(2,1)S(1)} %collective-permute-done.refs_0_, bf16[520,128]{1,0:T(8,128)(2,1)S(1)} %collective-permute-done.1.refs_1_, ...), custom_call_target="tpu_custom_call" | custom-call | tf_op jit(solution)/shard_map/pallas_call | solution.py:462
  23.1 0.0 copy-done
  23.1 1.6 %shard_map.92 = (bf16[128,1024]{1,0:T(8,128)(2,1)S(1)}, f32[128,1024]{1,0:T(8,128)S(1)}) custom-call(bf16[256,1024]{1,0:T(8,128)(2,1)S(1)} %get-tuple-element.28.refs_0_, f32[4,8,128]{2,1,0:T(8,128)S(1)} %get-tuple-element.29.refs_1_, bf16[256,1024]{1,0:T(8,128)(2,1)S(1)} %get-tuple-element.30.refs_2_, bf16[256,1024]{1,0:T(8,128)(2,1)S(1)} %get-tuple-element.31.refs_3_, ...), custom_call_target="tpu_custom_call" | custom-call | tf_op jit(solution)/shard_map/pallas_call | solution.py:470
  24.8 0.1 collective-permute-start.4
  24.9 0.0 collective-permute-done.6.refs_1_
  24.9 1.9 %shard_map.93 = (bf16[64,1024]{1,0:T(8,128)(2,1)S(1)}, f32[64,1024]{1,0:T(8,128)S(1)}) custom-call(bf16[520,128]{1,0:T(8,128)(2,1)S(1)} %collective-permute-done.5.refs_0_, bf16[520,128]{1,0:T(8,128)(2,1)S(1)} %collective-permute-done.6.refs_1_, f32[1,1024]{1,0:T(1,128)S(1)} %copy-done.4, bf16[1024,1024]{1,0:T(8,128)(2,1)S(1)} %bitcast.12, ...), custom_call_target="tpu_custom_call" | custom-call | tf_op jit(solution)/shard_map/pallas_call | solution.py:453
  26.8 0.5 %collective-permute-start.7 = (bf16[64,1024]{1,0:T(8,128)(2,1)S(1)}, bf16[64,1024]{1,0:T(8,128)(2,1)S(1)}, u32[]{:S(2)}, u32[]{:S(2)}) collective-permute-start(bf16[64,1024]{1,0:T(8,128)(2,1)S(1)} %get-tuple-element.38), channel_id=1, source_target_pairs={{0,1},{1,0},{2,3},{3,2},{4,5},{5,4},{6,7},{7,6},{8,9},{9,8},{10,11... | collective-permute-start | bytes 393224 | tf_op jit(solution)/shard_map/ppermute | solution.py:397
  27.3 0.0 collective-permute-done.9.refs_1_
  27.3 1.9 %shard_map.95 = (bf16[64,1024]{1,0:T(8,128)(2,1)S(1)}, f32[64,1024]{1,0:T(8,128)S(1)}) custom-call(bf16[520,128]{1,0:T(8,128)(2,1)S(1)} %collective-permute-done.8.refs_0_, bf16[520,128]{1,0:T(8,128)(2,1)S(1)} %collective-permute-done.9.refs_1_, f32[1,1024]{1,0:T(1,128)S(1)} %copy-done.4, bf16[1024,1024]{1,0:T(8,128)(2,1)S(1)} %bitcast.13, ...), custom_call_target="tpu_custom_call" | custom-call | tf_op jit(solution)/shard_map/pallas_call | solution.py:453
  29.3 0.1 collective-permute-start.10
  29.4 0.0 collective-permute-done.7.far_got
  29.4 0.0 collective-permute-done.4.near_got
  29.4 0.1 shard_map.94
  29.5 2.1 %collective-permute-start.11 = (bf16[64,1024]{1,0:T(8,128)(2,1)S(1)}, bf16[64,1024]{1,0:T(8,128)(2,1)S(1)}, u32[]{:S(2)}, u32[]{:S(2)}) collective-permute-start(bf16[64,1024]{1,0:T(8,128)(2,1)S(1)} %get-tuple-element.43), channel_id=1, source_target_pairs={{0,2},{1,3},{2,0},{3,1},{4,6},{5,7},{6,4},{7,5},{8,10},{9,11},{10,... | collective-permute-start | bytes 393224 | tf_op jit(solution)/shard_map/ppermute | solution.py:400
  31.6 0.0 collective-permute-done.10.far_got
  31.6 0.1 shard_map.96
  31.7 1.2 %collective-permute-start.12 = (bf16[64,1024]{1,0:T(8,128)(2,1)S(1)}, bf16[64,1024]{1,0:T(8,128)(2,1)S(1)}, u32[]{:S(2)}, u32[]{:S(2)}) collective-permute-start(bf16[64,1024]{1,0:T(8,128)(2,1)S(1)} %get-tuple-element.44), channel_id=1, source_target_pairs={{0,2},{1,3},{2,0},{3,1},{4,6},{5,7},{6,4},{7,5},{8,10},{9,11},{10,... | collective-permute-start | bytes 393224 | tf_op jit(solution)/shard_map/ppermute | solution.py:400
  32.8 3.1 %collective-permute-done.11.refs_2_ = bf16[64,1024]{1,0:T(8,128)(2,1)S(1)} collective-permute-done((bf16[64,1024]{1,0:T(8,128)(2,1)S(1)}, bf16[64,1024]{1,0:T(8,128)(2,1)S(1)}, u32[]{:S(2)}, u32[]{:S(2)}) %collective-permute-start.11) | collective-permute-done | bytes 131104 | tf_op jit(solution)/shard_map/ppermute | solution.py:400
  35.9 2.5 %collective-permute-done.12.refs_3_ = bf16[64,1024]{1,0:T(8,128)(2,1)S(1)} collective-permute-done((bf16[64,1024]{1,0:T(8,128)(2,1)S(1)}, bf16[64,1024]{1,0:T(8,128)(2,1)S(1)}, u32[]{:S(2)}, u32[]{:S(2)}) %collective-permute-start.12) | collective-permute-done | bytes 131104 | tf_op jit(solution)/shard_map/ppermute | solution.py:400
  38.5 0.8 %finish.1 = bf16[128,1024]{1,0:T(8,128)(2,1)} custom-call(f32[64,1024]{1,0:T(8,128)S(1)} %get-tuple-element.39.refs_0_, f32[64,1024]{1,0:T(8,128)S(1)} %get-tuple-element.42.refs_1_, bf16[64,1024]{1,0:T(8,128)(2,1)S(1)} %collective-permute-done.11.refs_2_, bf16[64,1024]{1,0:T(8,128)(2,1)S(1)} %collective-permute-done.12.refs_3_), custom_call_target="tpu_custom_call" | custom-call | tf_op jit(solution)/shard_map/finish/pallas_call | solution.py:502
Async XLA Ops:
  2.0 9.8 %collective-permute-start.5 = (bf16[520,128]{1,0:T(8,128)(2,1)S(1)}, bf16[520,128]{1,0:T(8,128)(2,1)S(1)}, u32[]{:S(2)}, u32[]{:S(2)}) collective-permute-start(bf16[520,128]{1,0:T(8,128)(2,1)S(1)} %get-tuple-element.36), channel_id=1, source_target_pairs={{0,28},{1,21},{2,26},{3,19},{4,24},{5,17},{6,30},{7,23},{8,20},{9,... | collective-permute-start | bytes 399368 | tf_op jit(solution)/shard_map/ppermute | solution.py:394
  8.0 9.7 %collective-permute-start = (bf16[520,128]{1,0:T(8,128)(2,1)S(1)}, bf16[520,128]{1,0:T(8,128)(2,1)S(1)}, u32[]{:S(2)}, u32[]{:S(2)}) collective-permute-start(bf16[520,128]{1,0:T(8,128)(2,1)S(1)} %get-tuple-element.25), channel_id=1, source_target_pairs={{0,12},{1,5},{2,14},{3,7},{4,8},{5,1},{6,10},{7,3},{8,4},{9,13},{1... | collective-permute-start | bytes 399368 | tf_op jit(solution)/shard_map/ppermute | solution.py:394
  11.8 5.9 %collective-permute-start.8 = (bf16[520,128]{1,0:T(8,128)(2,1)S(1)}, bf16[520,128]{1,0:T(8,128)(2,1)S(1)}, u32[]{:S(2)}, u32[]{:S(2)}) collective-permute-start(bf16[520,128]{1,0:T(8,128)(2,1)S(1)} %collective-permute-done.5.refs_0_), channel_id=1, source_target_pairs={{0,2},{1,3},{2,0},{3,1},{4,6},{5,7},{6,4},{7,5},{8,10},{9,11},{10,... | collective-permute-start | bytes 399368 | tf_op jit(solution)/shard_map/ppermute | solution.py:400
  12.3 4.9 %collective-permute-start.2 = (bf16[264,128]{1,0:T(8,128)(2,1)S(1)}, bf16[264,128]{1,0:T(8,128)(2,1)S(1)}, u32[]{:S(2)}, u32[]{:S(2)}) collective-permute-start(bf16[264,128]{1,0:T(8,128)(2,1)S(1)} %get-tuple-element.26), channel_id=1, source_target_pairs={{0,8},{1,9},{2,10},{3,11},{4,12},{5,13},{6,14},{7,15},{8,0},{9,1},... | collective-permute-start | bytes 202760 | tf_op jit(solution)/shard_map/ppermute | solution.py:394
  17.2 1.4 %collective-permute-start.3 = (bf16[264,128]{1,0:T(8,128)(2,1)S(1)}, bf16[264,128]{1,0:T(8,128)(2,1)S(1)}, u32[]{:S(2)}, u32[]{:S(2)}) collective-permute-start(bf16[264,128]{1,0:T(8,128)(2,1)S(1)} %collective-permute-done.2.refs_2_), channel_id=1, source_target_pairs={{0,1},{1,0},{2,3},{3,2},{4,5},{5,4},{6,7},{7,6},{8,9},{9,8},{10,11... | collective-permute-start | bytes 202760 | tf_op jit(solution)/shard_map/ppermute | solution.py:397
  17.2 7.7 %collective-permute-start.6 = (bf16[520,128]{1,0:T(8,128)(2,1)S(1)}, bf16[520,128]{1,0:T(8,128)(2,1)S(1)}, u32[]{:S(2)}, u32[]{:S(2)}) collective-permute-start(bf16[520,128]{1,0:T(8,128)(2,1)S(1)} %collective-permute-done.5.refs_0_), channel_id=1, source_target_pairs={{0,1},{1,0},{2,3},{3,2},{4,5},{5,4},{6,7},{7,6},{8,9},{9,8},{10,11... | collective-permute-start | bytes 399368 | tf_op jit(solution)/shard_map/ppermute | solution.py:397
  17.7 1.4 %collective-permute-start.1 = (bf16[520,128]{1,0:T(8,128)(2,1)S(1)}, bf16[520,128]{1,0:T(8,128)(2,1)S(1)}, u32[]{:S(2)}, u32[]{:S(2)}) collective-permute-start(bf16[520,128]{1,0:T(8,128)(2,1)S(1)} %collective-permute-done.refs_0_), channel_id=1, source_target_pairs={{0,1},{1,0},{2,3},{3,2},{4,5},{5,4},{6,7},{7,6},{8,9},{9,8},{10,11... | collective-permute-start | bytes 399368 | tf_op jit(solution)/shard_map/ppermute | solution.py:397
  17.7 9.6 %collective-permute-start.9 = (bf16[520,128]{1,0:T(8,128)(2,1)S(1)}, bf16[520,128]{1,0:T(8,128)(2,1)S(1)}, u32[]{:S(2)}, u32[]{:S(2)}) collective-permute-start(bf16[520,128]{1,0:T(8,128)(2,1)S(1)} %collective-permute-done.8.refs_0_), channel_id=1, source_target_pairs={{0,1},{1,0},{2,3},{3,2},{4,5},{5,4},{6,7},{7,6},{8,9},{9,8},{10,11... | collective-permute-start | bytes 399368 | tf_op jit(solution)/shard_map/ppermute | solution.py:397
  18.2 1.6 %copy-start.1 = (bf16[1,1024,1024]{2,1,0:T(8,128)(2,1)S(1)}, bf16[1,1024,1024]{2,1,0:T(8,128)(2,1)}, u32[]{:S(2)}) copy-start(bf16[1,1024,1024]{2,1,0:T(8,128)(2,1)} %param.13) | copy-start | bytes 6291460
  18.2 2.2 %copy-start.2 = (bf16[1,1024,1024]{2,1,0:T(8,128)(2,1)S(1)}, bf16[1,1024,1024]{2,1,0:T(8,128)(2,1)}, u32[]{:S(2)}) copy-start(bf16[1,1024,1024]{2,1,0:T(8,128)(2,1)} %param.14) | copy-start | bytes 6291460
  18.2 2.9 %copy-start.3 = (bf16[1,1024,1024]{2,1,0:T(8,128)(2,1)S(1)}, bf16[1,1024,1024]{2,1,0:T(8,128)(2,1)}, u32[]{:S(2)}) copy-start(bf16[1,1024,1024]{2,1,0:T(8,128)(2,1)} %param.15) | copy-start | bytes 6291460
  18.2 2.9 %copy-start.4 = (f32[1,1024]{1,0:T(1,128)S(1)}, f32[1,1024]{1,0:T(1,128)}, u32[]{:S(2)}) copy-start(f32[1,1024]{1,0:T(1,128)} %refs_2_.3) | copy-start | bytes 12292
  21.1 2.1 %copy-start = (bf16[1,1024,1024]{2,1,0:T(8,128)(2,1)S(1)}, bf16[1,1024,1024]{2,1,0:T(8,128)(2,1)}, u32[]{:S(2)}) copy-start(bf16[1,1024,1024]{2,1,0:T(8,128)(2,1)} %param.16) | copy-start | bytes 6291460
  24.8 4.6 %collective-permute-start.4 = (bf16[128,1024]{1,0:T(8,128)(2,1)S(1)}, bf16[128,1024]{1,0:T(8,128)(2,1)S(1)}, u32[]{:S(2)}, u32[]{:S(2)}) collective-permute-start(bf16[128,1024]{1,0:T(8,128)(2,1)S(1)} %get-tuple-element.35), channel_id=1, source_target_pairs={{0,1},{1,0},{2,3},{3,2},{4,5},{5,4},{6,7},{7,6},{8,9},{9,8},{10,11... | collective-permute-start | bytes 786440 | tf_op jit(solution)/shard_map/ppermute | solution.py:397
  26.8 2.6 %collective-permute-start.7 = (bf16[64,1024]{1,0:T(8,128)(2,1)S(1)}, bf16[64,1024]{1,0:T(8,128)(2,1)S(1)}, u32[]{:S(2)}, u32[]{:S(2)}) collective-permute-start(bf16[64,1024]{1,0:T(8,128)(2,1)S(1)} %get-tuple-element.38), channel_id=1, source_target_pairs={{0,1},{1,0},{2,3},{3,2},{4,5},{5,4},{6,7},{7,6},{8,9},{9,8},{10,11... | collective-permute-start | bytes 393224 | tf_op jit(solution)/shard_map/ppermute | solution.py:397
  29.3 2.3 %collective-permute-start.10 = (bf16[64,1024]{1,0:T(8,128)(2,1)S(1)}, bf16[64,1024]{1,0:T(8,128)(2,1)S(1)}, u32[]{:S(2)}, u32[]{:S(2)}) collective-permute-start(bf16[64,1024]{1,0:T(8,128)(2,1)S(1)} %get-tuple-element.41), channel_id=1, source_target_pairs={{0,1},{1,0},{2,3},{3,2},{4,5},{5,4},{6,7},{7,6},{8,9},{9,8},{10,11... | collective-permute-start | bytes 393224 | tf_op jit(solution)/shard_map/ppermute | solution.py:397
  29.5 6.5 %collective-permute-start.11 = (bf16[64,1024]{1,0:T(8,128)(2,1)S(1)}, bf16[64,1024]{1,0:T(8,128)(2,1)S(1)}, u32[]{:S(2)}, u32[]{:S(2)}) collective-permute-start(bf16[64,1024]{1,0:T(8,128)(2,1)S(1)} %get-tuple-element.43), channel_id=1, source_target_pairs={{0,2},{1,3},{2,0},{3,1},{4,6},{5,7},{6,4},{7,5},{8,10},{9,11},{10,... | collective-permute-start | bytes 393224 | tf_op jit(solution)/shard_map/ppermute | solution.py:400
  31.7 6.8 %collective-permute-start.12 = (bf16[64,1024]{1,0:T(8,128)(2,1)S(1)}, bf16[64,1024]{1,0:T(8,128)(2,1)S(1)}, u32[]{:S(2)}, u32[]{:S(2)}) collective-permute-start(bf16[64,1024]{1,0:T(8,128)(2,1)S(1)} %get-tuple-element.44), channel_id=1, source_target_pairs={{0,2},{1,3},{2,0},{3,1},{4,6},{5,7},{6,4},{7,5},{8,10},{9,11},{10,... | collective-permute-start | bytes 393224 | tf_op jit(solution)/shard_map/ppermute | solution.py:400
